TPU v7x, 256 devices: a whole 4x4x8 slice. The times are simulated.
256 devices in a mesh: plan: 32 (over x, y, core), draw: 8 (over z).
Axes of the slice: x: 4, y: 4, z: 8, core: 2. Of those that a mesh axis runs over, the one named last changes fastest.
Arguments:
- design: float32 [256, 128, 1024], P('plan', None, 'draw'), may hold values from 0 to 1
- class_ids: int32 [256, 128, 1024], P('plan', None, 'draw'), may hold values from 0 to 7
- class_radii: float32 [8, 3], replicated, may hold values from 0.5 to 16
- sensitivity: float32 [256, 128, 1024], P('plan', None, 'draw'), may hold values from -6 to 6
- row_patch: int32 [32, 8, 1024], P('plan', 'draw'), may hold values from 0 to 16383, as said below
Outputs:
- cast_density: float32 [256, 128, 1024], P('plan', None, 'draw')
- filtered_sens: float32 [256, 128, 1024], P('plan', None, 'draw')
- patch_sens: float32 [16384, 1024], P('plan', 'draw')
Inputs may be any that keep to these rules, and one draw needn't show every extreme that they name: `row_patch`: patch q belongs to plan tile q // 512. Of the rows of one device, at most 128 belong to the patches of any one plan tile; in every draw slab one plan tile gets exactly 128 rows from every device of that slab.
All inputs are finite; a program needn't handle non-finite values.
Results may differ from a plain program's by a relative error of at most 0.00017.
Values sent between devices are 32-bit elements; how exact they have to be, the bound alone decides.
A program may use at most 64 MiB of HBM per device.

v0:
```python
import jax
import jax.numpy as jnp
from jax import lax
from jax.sharding import PartitionSpec as P

PATCH_DEV = 512
SWEEPS = 16


BETA = 8.0
ETA = 0.5
RMIN = 0.2
POWER = 6.0


def extended(cells, sides, width):
    for axis, dim in sides:
        count = lax.axis_size(axis)
        ends = count - 1
        head = lax.slice_in_dim(cells, 0, width, axis=dim)
        tail = lax.slice_in_dim(cells, cells.shape[dim] - width, cells.shape[dim], axis=dim)
        cells = jnp.concatenate(
            [
                lax.ppermute(tail, axis, [(i, (i + 1) % count) for i in range(ends)]),
                cells,
                lax.ppermute(head, axis, [((i + 1) % count, i) for i in range(ends)]),
            ],
            axis=dim,
        )
    return cells


def entering(part, axis, combine, identity, reverse):
    count = lax.axis_size(axis)
    place = lax.axis_index(axis)
    ahead = count - 1 - place if reverse else place
    gathered = lax.all_gather(part, axis)
    state = jnp.zeros_like(part) + jnp.asarray(identity, part.dtype)

    def one(step, state):
        source = count - 1 - step if reverse else step
        return combine(state, lax.dynamic_index_in_dim(gathered, source, 0, False))

    return lax.fori_loop(0, ahead, one, state)


def coefficients(class_ids, class_radii):
    coef_x = jnp.zeros(class_ids.shape, jnp.float32)
    coef_y = jnp.zeros(class_ids.shape, jnp.float32)
    coef_z = jnp.zeros(class_ids.shape, jnp.float32)
    for level in range(class_radii.shape[0]):
        hit = class_ids == level
        coef_x = jnp.where(hit, class_radii[level, 0], coef_x)
        coef_y = jnp.where(hit, class_radii[level, 1], coef_y)
        coef_z = jnp.where(hit, class_radii[level, 2], coef_z)
    return (coef_x, coef_y, coef_z)


def relax(padded, coef_x, coef_y, coef_z, inv_diag, source):
    along_x = padded[2:, 1:-1, 1:-1] + padded[:-2, 1:-1, 1:-1]
    along_y = padded[1:-1, 2:, 1:-1] + padded[1:-1, :-2, 1:-1]
    along_z = padded[1:-1, 1:-1, 2:] + padded[1:-1, 1:-1, :-2]
    return (source + coef_x * along_x + coef_y * along_y + coef_z * along_z) * inv_diag


def pad_second(field):
    return jnp.pad(field, ((0, 0), (1, 1), (0, 0)))


def smooth_each(source, coef_x, coef_y, coef_z, inv_diag):

    def sweep(index, field):
        wider = extended(field, (("plan", 0), ("draw", 2)), 1)
        return relax(pad_second(wider), coef_x, coef_y, coef_z, inv_diag, source)

    return lax.fori_loop(0, SWEEPS, sweep, source)


def per_device(design, class_ids, class_radii, sensitivity, row_patch):
    coef_x, coef_y, coef_z = coefficients(class_ids, class_radii)
    inv_diag = 1.0 / (1.0 + 2.0 * (coef_x + coef_y + coef_z))
    filtered = smooth_each(design, coef_x, coef_y, coef_z, inv_diag)
    denom = jnp.tanh(jnp.float32(BETA * ETA)) + jnp.tanh(jnp.float32(BETA * (1.0 - ETA)))
    steep = jnp.tanh(BETA * (filtered - ETA))
    projected = RMIN + (1.0 - RMIN) * (jnp.tanh(jnp.float32(BETA * ETA)) + steep) / denom
    running = jnp.cumsum(jnp.power(projected, POWER), axis=2)
    totals = running[:, :, -1]
    carried = entering(
        totals, "draw", lambda first, second: first + second, jnp.zeros_like(totals), False
    )
    prefix = running + carried[:, :, None]
    cast_density = jnp.power(prefix, 1.0 / POWER)
    weighted = sensitivity * jnp.power(prefix, (1.0 - POWER) / POWER)
    backward = jnp.flip(jnp.cumsum(jnp.flip(weighted, 2), axis=2), 2)
    rests = backward[:, :, 0]
    below = entering(
        rests, "draw", lambda first, second: first + second, jnp.zeros_like(rests), True
    )
    suffix = backward + below[:, :, None]
    chained = (
        jnp.power(projected, POWER - 1.0)
        * suffix
        * (1.0 - RMIN)
        * BETA
        * (1.0 - steep * steep)
        / denom
    )
    filtered_sens = smooth_each(chained, coef_x, coef_y, coef_z, inv_diag)
    depth = filtered_sens.shape[2]
    row_count = filtered_sens.shape[0] * filtered_sens.shape[1]
    tiles = lax.axis_size("plan")
    capacity = 4 * row_count // tiles
    row_data = filtered_sens.reshape(row_count, depth)
    patch_ids = row_patch.reshape(row_count)
    owners = patch_ids // PATCH_DEV
    slot_patch = patch_ids - owners * PATCH_DEV
    onehot = (owners[:, None] == jnp.arange(tiles, dtype=jnp.int32)[None, :]).astype(jnp.int32)
    ranking = jnp.sum(jnp.cumsum(onehot, axis=0) * onehot, axis=1) - 1
    position = owners * capacity + ranking
    sendbuf = jnp.zeros((tiles * capacity, depth), jnp.float32).at[position].set(row_data)
    send_ids = (
        jnp.full((tiles * capacity,), float(PATCH_DEV), jnp.float32)
        .at[position]
        .set(slot_patch.astype(jnp.float32))
    )
    arrived, arrived_ids = (
        lax.all_to_all(
            sendbuf.reshape(tiles, capacity, depth), "plan", split_axis=0, concat_axis=0, tiled=True
        ),
        lax.all_to_all(
            send_ids.reshape(tiles, capacity), "plan", split_axis=0, concat_axis=0, tiled=True
        ),
    )
    summed = jax.ops.segment_sum(
        arrived.reshape(tiles * capacity, depth),
        arrived_ids.reshape(tiles * capacity).astype(jnp.int32),
        num_segments=PATCH_DEV + 1,
    )
    patch_sens = 0.25 * summed[:PATCH_DEV]
    return (cast_density, filtered_sens, patch_sens)


def solution(mesh):
    in_specs = (
        P("plan", None, "draw"),
        P("plan", None, "draw"),
        P(),
        P("plan", None, "draw"),
        P("plan", "draw", None),
    )
    out_specs = (P("plan", None, "draw"), P("plan", None, "draw"), P("plan", "draw"))
    return jax.shard_map(
        per_device, mesh=mesh, in_specs=in_specs, out_specs=out_specs, check_vma=False
    )
```

profile of v0, /device:TPU:1, one launch (start us, length us, event | category | flops | bytes accessed | tf_op | source)
XLA Modules:
  0.0 895.7 jit_solution(7360819999949229405)
XLA Ops:
  1.4 9.0 %reduce-window.6 = s32[32,8,128]{2,1,0:T(8,128)S(1)} reduce-window(s32[32,8,128]{2,1,0:T(8,128)S(1)} %fusion.37, s32[]{:T(128)} %copy.149), window={size=1x1x128 pad=0_0x0_0x127_0}, to_apply=%region_10.11 | reduce-window | flops 4161536 | bytes 262148 | tf_op jit(solution)/shard_map/reduce-window
  12.4 4.9 scatter_custom_fusion
  17.3 8.6 all-to-all-start
  34.3 15.7 %add_divide_fusion = (f32[8,128,128]{1,0,2:T(8,128)S(1)}, f32[8,128,128]{1,0,2:T(8,128)S(1)}, f32[8,128,128]{1,0,2:T(8,128)S(1)}, f32[8,128,128]{1,0,2:T(8,128)S(1)}) fusion(pred[8,128,128]{1,0,2:T(8,128)(4,1)S(1)} %get-tuple-element.397, pred[8,128,128]{1,0,2:T(8,128)(4,1)S(1)} %get-tuple-element.396, pred[8,128,128]{1,0,2:T(8,128)(4,1)S(1)} %get-tuple-element.395, ...), kind=kLoop, calls=%fused_computation.59 | loop fusion | flops 3801088 | bytes 3145824 | tf_op jit(solution)/shard_map/div | solution.py:81
  50.4 348.7 %while.46 = (s32[]{:T(128)}, f32[8,128,128]{1,2,0:T(8,128)}, f32[8,128,128]{1,2,0:T(8,128)S(1)}, f32[8,128,128]{1,2,0:T(8,128)}, f32[8,128,128]{1,2,0:T(8,128)S(...) while((s32[]{:T(128)}, f32[8,128,128]{1,2,0:T(8,128)}, ...), condition=%wide.region_1.2_spmd, body=%wide.region_0.1_spmd.sunk | while | flops 3187010 | bytes 10064277 | solution.py:76
  86.2 4.4 collective-permute-done.3
  103.1 4.8 collective-permute-start.2
  162.4 5.0 collective-permute-done.1
  178.8 3.8 collective-permute-start
  184.5 5.0 collective-permute-done.1
  200.9 3.8 collective-permute-start
  206.7 5.0 collective-permute-done.1
  223.0 3.8 collective-permute-start
  228.8 5.0 collective-permute-done.1
  245.2 3.8 collective-permute-start
  250.9 5.0 collective-permute-done.1
  273.1 5.0 collective-permute-done.1
  295.2 5.0 collective-permute-done.1
  317.4 5.0 collective-permute-done.1
  339.5 5.0 collective-permute-done.1
  361.7 5.0 collective-permute-done.1
  383.8 5.0 collective-permute-done.1
  400.7 18.1 %all-gather = f32[64,128,1]{1,0,2:T(8,128)S(1)} all-gather(f32[8,128,1]{1,0,2:T(8,128)S(1)} %slice.265), channel_id=2, replica_groups=mesh['plan'=32,'draw'=8] {'draw'}, dimensions={0}, use_global_device_ids=true | all-gather | bytes 36864 | tf_op jit(solution)/shard_map/all_gather | solution.py:37
  421.3 23.3 %fusion.56 = f32[8,128,128]{1,0,2:T(8,128)S(1)} fusion(f32[8,128,128]{1,0,2:T(8,128)S(1)} %rev.7), kind=kOutput, calls=%fused_computation.124 | output fusion | flops 16646144 | bytes 1048576 | tf_op jit(solution)/shard_map/jit(cumsum)/reduce_window_sum | solution.py:94
  444.6 18.1 %all-gather.1 = f32[64,128,1]{1,0,2:T(8,128)S(1)} all-gather(f32[8,128,1]{1,0,2:T(8,128)S(1)} %slice.266), channel_id=3, replica_groups=mesh['plan'=32,'draw'=8] {'draw'}, dimensions={0}, use_global_device_ids=true | all-gather | bytes 36864 | tf_op jit(solution)/shard_map/all_gather | solution.py:37
  465.5 351.2 %while.49 = (s32[]{:T(128)}, f32[8,128,128]{1,2,0:T(8,128)}, f32[8,128,128]{1,2,0:T(8,128)S(1)}, f32[8,128,128]{1,2,0:T(8,128)}, f32[8,128,128]{1,2,0:T(8,128)S(...) while((s32[]{:T(128)}, f32[8,128,128]{1,2,0:T(8,128)}, ...), condition=%wide.region_9.10_spmd, body=%wide.region_8.9_spmd.sunk | while | flops 3187010 | bytes 12161457 | solution.py:76
  466.6 16.5 %collective-permute-start.4 = (f32[1,128,128]{1,2,0:T(8,128)S(1)}, f32[1,128,128]{1,2,0:T(8,128)S(1)}, u32[]{:S(2)}, u32[]{:S(2)}) collective-permute-start(f32[1,128,128]{1,2,0:T(8,128)S(1)} %get-tuple-element.574), channel_id=1, source_target_pairs={{0,8},{8,16},{16,24},{24,32},{32,40},{40,48},{48,56},{56,64},{64,7... | collective-permute-start | bytes 196616 | tf_op jit(solution)/shard_map/while/body/eval_jaxpr/ppermute | solution.py:24
  498.1 5.4 collective-permute-start.4
  519.4 5.1 collective-permute-start.4
  541.2 5.1 collective-permute-start.4
  548.3 5.3 collective-permute-done.5
  564.2 4.0 collective-permute-start.4
  570.2 5.0 collective-permute-done.5
  591.3 5.0 collective-permute-done.5
  612.4 5.0 collective-permute-done.5
  633.6 5.0 collective-permute-done.5
  654.7 5.0 collective-permute-done.5
  675.8 5.0 collective-permute-done.5
  696.9 5.0 collective-permute-done.5
  718.0 5.0 collective-permute-done.5
  739.1 5.0 collective-permute-done.5
  760.2 5.0 collective-permute-done.5
  781.3 5.0 collective-permute-done.5
  802.4 5.0 collective-permute-done.5
  818.0 4.5 scatter_custom_fusion.1
  822.5 17.5 %all-to-all-start.1 = ((f32[32,128,128]{2,1,0:T(8,128)}), f32[32,128,128]{2,1,0:T(8,128)S(1)}, u32[]{:S(2)}, u32[]{:S(2)}) async-start(f32[32,128,128]{2,1,0:T(8,128)} %bitcast.38), calls=%async_computation.1 | async-start | bytes 4194304 | tf_op jit(solution)/shard_map/all_to_all | solution.py:127
  841.0 27.2 %all-to-all-done.1 = f32[32,128,128]{2,1,0:T(8,128)S(1)} async-done(((f32[32,128,128]{2,1,0:T(8,128)}), f32[32,128,128]{2,1,0:T(8,128)S(1)}, u32[]{:S(2)}, u32[]{:S(2)}) %all-to-all-start.1) | async-done | bytes 2097184 | tf_op jit(solution)/shard_map/all_to_all | solution.py:127
  868.3 26.7 %scatter_custom_fusion.2 = f32[513,128]{1,0:T(8,128)S(1)} fusion(s32[4096]{0:T(1024)S(1)} %bitcast.77, f32[4096,128]{1,0:T(8,128)S(1)} %bitcast.68, f32[]{:T(128)} %constant.131.clone.1), kind=kCustom, calls=%fused_computation.79 | custom fusion | flops 524288 | bytes 262660 | tf_op jit(solution)/shard_map/scatter-add | solution.py:134
  (570 shorter events, 538.8 us)
Async XLA Ops:
  17.3 805.2 %all-to-all-start = ((f32[32,1,128]{2,1,0:T(1,128)}), f32[32,1,128]{2,1,0:T(1,128)S(1)}, u32[]{:S(2)}, u32[]{:S(2)}) async-start(f32[32,1,128]{2,1,0:T(1,128)} %bitcast.35), calls=%async_computation | async-start | bytes 32768 | tf_op jit(solution)/shard_map/all_to_all | solution.py:130
  103.1 6.2 collective-permute-start.2
  160.4 7.0 collective-permute-start.1
  178.8 5.7 collective-permute-start
  182.5 7.0 collective-permute-start.1
  200.9 5.7 collective-permute-start
  204.7 7.0 collective-permute-start.1
  223.0 5.7 collective-permute-start
  226.8 7.0 collective-permute-start.1
  245.2 5.7 collective-permute-start
  248.9 7.0 collective-permute-start.1
  267.3 5.7 collective-permute-start
  271.1 7.0 collective-permute-start.1
  289.5 5.7 collective-permute-start
  293.2 7.0 collective-permute-start.1
  311.6 5.7 collective-permute-start
  315.4 7.0 collective-permute-start.1
  333.8 5.7 collective-permute-start
  337.5 7.0 collective-permute-start.1
  355.9 5.7 collective-permute-start
  359.7 7.0 collective-permute-start.1
  378.0 5.7 collective-permute-start
  381.8 7.0 collective-permute-start.1
  466.6 18.4 %collective-permute-start.4 = (f32[1,128,128]{1,2,0:T(8,128)S(1)}, f32[1,128,128]{1,2,0:T(8,128)S(1)}, u32[]{:S(2)}, u32[]{:S(2)}) collective-permute-start(f32[1,128,128]{1,2,0:T(8,128)S(1)} %get-tuple-element.574), channel_id=1, source_target_pairs={{0,8},{8,16},{16,24},{24,32},{32,40},{40,48},{48,56},{56,64},{64,7... | collective-permute-start | bytes 196616 | tf_op jit(solution)/shard_map/while/body/eval_jaxpr/ppermute | solution.py:24
  498.1 7.3 collective-permute-start.4
  519.4 7.0 collective-permute-start.4
  541.2 7.0 collective-permute-start.4
  546.3 7.3 collective-permute-start.5
  564.2 5.9 collective-permute-start.4
  568.2 7.0 collective-permute-start.5
  585.6 5.7 collective-permute-start.4
  589.3 7.0 collective-permute-start.5
  606.7 5.7 collective-permute-start.4
  610.5 7.0 collective-permute-start.5
  627.8 5.7 collective-permute-start.4
  631.6 7.0 collective-permute-start.5
  648.9 5.7 collective-permute-start.4
  652.7 7.0 collective-permute-start.5
  670.0 5.7 collective-permute-start.4
  673.8 7.0 collective-permute-start.5
  691.1 5.7 collective-permute-start.4
  694.9 7.0 collective-permute-start.5
  716.0 7.0 collective-permute-start.5
  737.1 7.0 collective-permute-start.5
  758.2 7.0 collective-permute-start.5
  779.3 7.0 collective-permute-start.5
  800.4 7.0 collective-permute-start.5
  822.5 45.8 %all-to-all-start.1 = ((f32[32,128,128]{2,1,0:T(8,128)}), f32[32,128,128]{2,1,0:T(8,128)S(1)}, u32[]{:S(2)}, u32[]{:S(2)}) async-start(f32[32,128,128]{2,1,0:T(8,128)} %bitcast.38), calls=%async_computation.1 | async-start | bytes 4194304 | tf_op jit(solution)/shard_map/all_to_all | solution.py:127
  (105 other events, 546.8 us)
where the time goes:
time: 902 us; the launch traced here: 896 us
  starting transfers between devices  366 us (41%)
  waiting for transfers between devices  275 us (30%)
  other arithmetic  157 us (17%)
  local copies, waits for them, and re-layouts  57.8 us (6%)
  blocking collectives  36.2 us (4%)
    ppermute x64, waiting for transfers between devices, extended(): lax.ppermute(head, axis, [((i + 1) % count, i) for i in range(ends)])  248 us
    ppermute x64, starting transfers between devices, extended(): lax.ppermute(tail, axis, [(i, (i + 1) % count) for i in range(ends)])  237 us
    ppermute x64, starting transfers between devices, extended(): lax.ppermute(head, axis, [((i + 1) % count, i) for i in range(ends)])  103 us
    mul x32, other arithmetic, relax(): (source + coef_x * along_x + coef_y * along_y + coef_z * along_z) * inv_diag  59 us
    all_gather x2, blocking collectives, entering(): gathered = lax.all_gather(part, axis)  36.2 us
    while x128, local copies, waits for them, and re-layouts  34.8 us
    all_to_all x1, waiting for transfers between devices, per_device(): lax.all_to_all(sendbuf.reshape(tiles, capacity, depth), 'plan', split_axi...  27.2 us
    scatter-add x1, other arithmetic, per_device(): jax.ops.segment_sum(arrived.reshape(tiles * capacity, depth), arrived_ids...  26.7 us
  transfers between devices with their start and end apart: 130, of which 65 were waited for; matrix products, arithmetic and copies ran while one was open for 19% of the time, Pallas kernels for 0%

commit v1 on v0

--- a/solution.py
+++ b/solution.py
@@ -1,33 +1,22 @@
+import functools
+
 import jax
 import jax.numpy as jnp
 from jax import lax
+from jax.experimental import pallas as pl
+from jax.experimental.pallas import tpu as pltpu
 from jax.sharding import PartitionSpec as P
 
 PATCH_DEV = 512
 SWEEPS = 16
-
+HALO = 8
 
 BETA = 8.0
 ETA = 0.5
 RMIN = 0.2
 POWER = 6.0
 
-
-def extended(cells, sides, width):
-    for axis, dim in sides:
-        count = lax.axis_size(axis)
-        ends = count - 1
-        head = lax.slice_in_dim(cells, 0, width, axis=dim)
-        tail = lax.slice_in_dim(cells, cells.shape[dim] - width, cells.shape[dim], axis=dim)
-        cells = jnp.concatenate(
-            [
-                lax.ppermute(tail, axis, [(i, (i + 1) % count) for i in range(ends)]),
-                cells,
-                lax.ppermute(head, axis, [((i + 1) % count, i) for i in range(ends)]),
-            ],
-            axis=dim,
-        )
-    return cells
+MESH = pl.DeviceIdType.MESH
 
 
 def entering(part, axis, combine, identity, reverse):
@@ -56,47 +45,134 @@
     return (coef_x, coef_y, coef_z)
 
 
-def relax(padded, coef_x, coef_y, coef_z, inv_diag, source):
-    along_x = padded[2:, 1:-1, 1:-1] + padded[:-2, 1:-1, 1:-1]
-    along_y = padded[1:-1, 2:, 1:-1] + padded[1:-1, :-2, 1:-1]
-    along_z = padded[1:-1, 1:-1, 2:] + padded[1:-1, 1:-1, :-2]
-    return (source + coef_x * along_x + coef_y * along_y + coef_z * along_z) * inv_diag
-
-
-def pad_second(field):
-    return jnp.pad(field, ((0, 0), (1, 1), (0, 0)))
-
-
-def smooth_each(source, coef_x, coef_y, coef_z, inv_diag):
-
-    def sweep(index, field):
-        wider = extended(field, (("plan", 0), ("draw", 2)), 1)
-        return relax(pad_second(wider), coef_x, coef_y, coef_z, inv_diag, source)
-
-    return lax.fori_loop(0, SWEEPS, sweep, source)
-
-
-def per_device(design, class_ids, class_radii, sensitivity, row_patch):
-    coef_x, coef_y, coef_z = coefficients(class_ids, class_radii)
+def filter_kernel(n_plan, n_draw, src_ref, cx_ref, cy_ref, cz_ref, inv_ref, out_ref, field, send_sem, recv_sem):
+    planes, depth, width = src_ref.shape
+    p = lax.axis_index("plan")
+    d = lax.axis_index("draw")
+    has_l = p > 0
+    has_r = p < n_plan - 1
+    has_b = d > 0
+    has_a = d < n_draw - 1
+    lo = HALO
+    hi = HALO + depth
+
+    field[...] = jnp.zeros_like(field)
+    for i in range(planes):
+        field[0, i + 1, pl.ds(lo, depth), :] = src_ref[i]
+
+    barrier = pltpu.get_barrier_semaphore()
+    neighbours = ((has_l, (p - 1, d)), (has_r, (p + 1, d)), (has_b, (p, d - 1)), (has_a, (p, d + 1)))
+    for cond, dev in neighbours:
+        @pl.when(cond)
+        def _():
+            pl.semaphore_signal(barrier, 1, device_id=dev, device_id_type=MESH)
+    peers = sum(cond.astype(jnp.int32) for cond, _ in neighbours)
+    pl.semaphore_wait(barrier, peers)
+
+    def copies(s):
+        to_l = pltpu.make_async_remote_copy(
+            field.at[s, 1, pl.ds(lo, depth), :], field.at[s, planes + 1, pl.ds(lo, depth), :],
+            send_sem.at[s, 0], recv_sem.at[s, 0], device_id=(p - 1, d), device_id_type=MESH)
+        to_r = pltpu.make_async_remote_copy(
+            field.at[s, planes, pl.ds(lo, depth), :], field.at[s, 0, pl.ds(lo, depth), :],
+            send_sem.at[s, 1], recv_sem.at[s, 1], device_id=(p + 1, d), device_id_type=MESH)
+        to_b = pltpu.make_async_remote_copy(
+            field.at[s, pl.ds(1, planes), pl.ds(lo, HALO), :], field.at[s, pl.ds(1, planes), pl.ds(hi, HALO), :],
+            send_sem.at[s, 2], recv_sem.at[s, 2], device_id=(p, d - 1), device_id_type=MESH)
+        to_a = pltpu.make_async_remote_copy(
+            field.at[s, pl.ds(1, planes), pl.ds(hi - HALO, HALO), :], field.at[s, pl.ds(1, planes), pl.ds(0, HALO), :],
+            send_sem.at[s, 3], recv_sem.at[s, 3], device_id=(p, d + 1), device_id_type=MESH)
+        return ((to_l, has_l, has_r), (to_r, has_r, has_l), (to_b, has_b, has_a), (to_a, has_a, has_b))
+
+    def exchange(s):
+        group = copies(s)
+        for copy, send, _ in group:
+            @pl.when(send)
+            def _():
+                copy.start()
+        for copy, send, recv in group:
+            @pl.when(send)
+            def _():
+                copy.wait_send()
+
+            @pl.when(recv)
+            def _():
+                copy.wait_recv()
+
+    lane = lax.broadcasted_iota(jnp.int32, (depth, width), 1)
+
+    def sweep(s, last):
+        t = 1 - s
+        for i in range(planes):
+            c = field[s, i + 1, pl.ds(lo, depth), :]
+            zm = field[s, i + 1, pl.ds(lo - 1, depth), :]
+            zp = field[s, i + 1, pl.ds(lo + 1, depth), :]
+            xm = field[s, i, pl.ds(lo, depth), :]
+            xp = field[s, i + 2, pl.ds(lo, depth), :]
+            ym = jnp.where(lane == 0, 0.0, pltpu.roll(c, 1, 1))
+            yp = jnp.where(lane == width - 1, 0.0, pltpu.roll(c, width - 1, 1))
+            new = (src_ref[i] + cx_ref[i] * (xm + xp) + cy_ref[i] * (ym + yp) + cz_ref[i] * (zm + zp)) * inv_ref[i]
+            if last:
+                out_ref[i] = new
+            else:
+                field[t, i + 1, pl.ds(lo, depth), :] = new
+
+    exchange(0)
+
+    def pair(k, carry):
+        sweep(0, False)
+        exchange(1)
+        sweep(1, False)
+        exchange(0)
+        return carry
+
+    lax.fori_loop(0, SWEEPS // 2 - 1, pair, 0)
+    sweep(0, False)
+    exchange(1)
+    sweep(1, True)
+
+
+def smooth_each(source, coef_x, coef_y, coef_z, inv_diag, n_plan, n_draw, kid):
+    planes, depth, width = source.shape
+    vmem = pl.BlockSpec(memory_space=pltpu.VMEM)
+    return pl.pallas_call(
+        functools.partial(filter_kernel, n_plan, n_draw),
+        out_shape=jax.ShapeDtypeStruct(source.shape, jnp.float32),
+        in_specs=[vmem] * 5,
+        out_specs=vmem,
+        scratch_shapes=[
+            pltpu.VMEM((2, planes + 2, depth + 2 * HALO, width), jnp.float32),
+            pltpu.SemaphoreType.DMA((2, 4)),
+            pltpu.SemaphoreType.DMA((2, 4)),
+        ],
+        compiler_params=pltpu.CompilerParams(collective_id=kid, has_side_effects=True),
+    )(source, coef_x, coef_y, coef_z, inv_diag)
+
+
+def per_device(n_plan, n_draw, design, class_ids, class_radii, sensitivity, row_patch):
+    design_t = jnp.swapaxes(design, 1, 2)
+    ids_t = jnp.swapaxes(class_ids, 1, 2)
+    sens_t = jnp.swapaxes(sensitivity, 1, 2)
+    coef_x, coef_y, coef_z = coefficients(ids_t, class_radii)
     inv_diag = 1.0 / (1.0 + 2.0 * (coef_x + coef_y + coef_z))
-    filtered = smooth_each(design, coef_x, coef_y, coef_z, inv_diag)
+    filtered = smooth_each(design_t, coef_x, coef_y, coef_z, inv_diag, n_plan, n_draw, 0)
     denom = jnp.tanh(jnp.float32(BETA * ETA)) + jnp.tanh(jnp.float32(BETA * (1.0 - ETA)))
     steep = jnp.tanh(BETA * (filtered - ETA))
     projected = RMIN + (1.0 - RMIN) * (jnp.tanh(jnp.float32(BETA * ETA)) + steep) / denom
-    running = jnp.cumsum(jnp.power(projected, POWER), axis=2)
-    totals = running[:, :, -1]
+    running = jnp.cumsum(jnp.power(projected, POWER), axis=1)
+    totals = running[:, -1, :]
     carried = entering(
         totals, "draw", lambda first, second: first + second, jnp.zeros_like(totals), False
     )
-    prefix = running + carried[:, :, None]
+    prefix = running + carried[:, None, :]
     cast_density = jnp.power(prefix, 1.0 / POWER)
-    weighted = sensitivity * jnp.power(prefix, (1.0 - POWER) / POWER)
-    backward = jnp.flip(jnp.cumsum(jnp.flip(weighted, 2), axis=2), 2)
-    rests = backward[:, :, 0]
+    weighted = sens_t * jnp.power(prefix, (1.0 - POWER) / POWER)
+    backward = jnp.flip(jnp.cumsum(jnp.flip(weighted, 1), axis=1), 1)
+    rests = backward[:, 0, :]
     below = entering(
         rests, "draw", lambda first, second: first + second, jnp.zeros_like(rests), True
     )
-    suffix = backward + below[:, :, None]
+    suffix = backward + below[:, None, :]
     chained = (
         jnp.power(projected, POWER - 1.0)
         * suffix
@@ -105,7 +181,9 @@
         * (1.0 - steep * steep)
         / denom
     )
-    filtered_sens = smooth_each(chained, coef_x, coef_y, coef_z, inv_diag)
+    filtered_sens_t = smooth_each(chained, coef_x, coef_y, coef_z, inv_diag, n_plan, n_draw, 1)
+    filtered_sens = jnp.swapaxes(filtered_sens_t, 1, 2)
+    cast_density = jnp.swapaxes(cast_density, 1, 2)
     depth = filtered_sens.shape[2]
     row_count = filtered_sens.shape[0] * filtered_sens.shape[1]
     tiles = lax.axis_size("plan")
@@ -150,5 +228,6 @@
     )
     out_specs = (P("plan", None, "draw"), P("plan", None, "draw"), P("plan", "draw"))
     return jax.shard_map(
-        per_device, mesh=mesh, in_specs=in_specs, out_specs=out_specs, check_vma=False
-    )
+        functools.partial(per_device, mesh.shape["plan"], mesh.shape["draw"]),
+        mesh=mesh, in_specs=in_specs, out_specs=out_specs, check_vma=False
+    )

time: 902 us -> 343 us (0.38)
  starting transfers between devices: 366 us -> 26 us
  waiting for transfers between devices: 275 us -> 27.3 us
  Pallas kernels: 0 us -> 150 us
  other arithmetic: 157 us -> 83.3 us
  local copies, waits for them, and re-layouts: 57.8 us -> 18.4 us
    ppermute x128 -> x0, starting transfers between devices: 339 us -> none  [the longest x64 237 us: extended(): lax.ppermute(tail, axis, [(i, (i + 1) % count) for i in range(ends)])]
    ppermute x128 -> x0, waiting for transfers between devices: 248 us -> none  [the longest x64 248 us: extended(): lax.ppermute(head, axis, [((i + 1) % count, i) for i in range(ends)])]
    pallas_call x0 -> x2, Pallas kernels: none -> 150 us  [smooth_each(): pl.pallas_call(functools.partial(filter_kernel, n_plan, n_draw), out_shap...]
    mul x33 -> x1, other arithmetic: 60.4 us -> 0.43 us  [per_device(): weighted = sens_t * jnp.power(prefix, (1.0 - POWER) / POWER)]
    while x134 -> x0, local copies, waits for them, and re-layouts: 36.3 us -> none
    concatenate x32 -> x0, other arithmetic: 15.1 us -> none  [extended(): jnp.concatenate([lax.ppermute(tail, axis, [(i, (i + 1) % count) for i in...]
  transfers between devices with their start and end apart: 130 -> 2, of which waited for: 65 -> 1; matrix products, arithmetic and copies ran while one was open for 19% -> 17% of each run, Pallas kernels for 0% -> 44%
where the time goes in v1:
time: 343 us
  Pallas kernels  150 us (44%)
  other arithmetic  83.3 us (24%)
  blocking collectives  36.4 us (11%)
  waiting for transfers between devices  27.3 us (8%)
  starting transfers between devices  26 us (8%)
  local copies, waits for them, and re-layouts  18.4 us (5%)
    pallas_call x2, Pallas kernels, smooth_each(): pl.pallas_call(functools.partial(filter_kernel, n_plan, n_draw), out_shap...  150 us
    all_gather x2, blocking collectives, entering(): gathered = lax.all_gather(part, axis)  36.4 us
    all_to_all x1, waiting for transfers between devices, per_device(): lax.all_to_all(sendbuf.reshape(tiles, capacity, depth), 'plan', split_axi...  27.2 us
    scatter-add x1, other arithmetic, per_device(): jax.ops.segment_sum(arrived.reshape(tiles * capacity, depth), arrived_ids...  26.7 us
    another operation x1, other arithmetic, per_device(): backward = jnp.flip(jnp.cumsum(jnp.flip(weighted, 1), axis=1), 1)  23.3 us
    all_to_all x1, starting transfers between devices, per_device(): lax.all_to_all(sendbuf.reshape(tiles, capacity, depth), 'plan', split_axi...  17.4 us
    div x1, other arithmetic, per_device(): inv_diag = 1.0 / (1.0 + 2.0 * (coef_x + coef_y + coef_z))  17.4 us
    another operation x3, other arithmetic  9.15 us
  transfers between devices with their start and end apart: 2, of which 1 were waited for; matrix products, arithmetic and copies ran while one was open for 17% of the time, Pallas kernels for 44%

profile of v1, /device:TPU:1, one launch (start us, length us, event | category | flops | bytes accessed | tf_op | source)
XLA Modules:
  0.0 342.6 jit_solution(13943734490766963671)
XLA Ops:
  0.6 0.0 copy-start.1
  0.6 0.8 add_select_fusion
  1.4 9.0 %reduce-window.6 = s32[32,8,128]{2,1,0:T(8,128)S(1)} reduce-window(s32[32,8,128]{2,1,0:T(8,128)S(1)} %fusion.9, s32[]{:T(128)} %constant.100.clone.1), window={size=1x1x128 pad=0_0x0_0x127_0}, to_apply=%region_6.7 | reduce-window | flops 4161536 | bytes 262148 | tf_op jit(solution)/shard_map/reduce-window
  10.4 0.1 slice.119
  10.5 0.1 copy.34
  10.7 0.1 copy.35
  10.8 0.1 broadcast_add_fusion
  10.9 0.7 subtract_convert_fusion
  11.6 0.7 compare_select_fusion
  12.4 4.9 %scatter_custom_fusion = f32[4096]{0:T(1024)} fusion(s32[1024]{0:T(1024)S(1)} %bitcast.95, f32[1024]{0:T(1024)S(1)} %get-tuple-element.120, f32[]{:T(128)} %constant.116.clone.1), kind=kCustom, calls=%fused_computation.42 | custom fusion | bytes 16388 | tf_op jit(solution)/shard_map/scatter | solution.py:202
  17.2 8.6 %all-to-all-start = ((f32[32,1,128]{2,1,0:T(1,128)}), f32[32,1,128]{2,1,0:T(1,128)S(1)}, u32[]{:S(2)}, u32[]{:S(2)}) async-start(f32[32,1,128]{2,1,0:T(1,128)} %bitcast.42), calls=%async_computation | async-start | bytes 32768 | tf_op jit(solution)/shard_map/all_to_all | solution.py:208
  25.8 2.1 fusion.16
  27.9 1.5 fusion.17
  29.5 1.2 copy.23
  30.7 0.7 broadcast_compare_fusion
  31.4 0.0 copy-done.1
  31.4 1.0 copy.22
  32.4 17.4 %add_divide_fusion = (f32[8,128,128]{2,1,0:T(8,128)}, f32[8,128,128]{2,1,0:T(8,128)}, f32[8,128,128]{2,1,0:T(8,128)}, f32[8,128,128]{2,1,0:T(8,128)}) fusion(pred[8,128,128]{1,2,0:T(8,128)(4,1)S(1)} %get-tuple-element.119, pred[8,128,128]{1,2,0:T(8,128)(4,1)S(1)} %get-tuple-element.118, pred[8,128,128]{1,2,0:T(8,128)(4,1)S(1)} %get-tuple-element.117, ...), kind=kLoop, calls=%fused_computation.18 | loop fusion | flops 3801088 | bytes 3145824 | tf_op jit(solution)/shard_map/div | solution.py:157
  49.8 0.0 copy-start.2
  49.8 68.8 %shard_map.76 = f32[8,128,128]{2,1,0:T(8,128)} custom-call(f32[8,128,128]{2,1,0:T(8,128)} %bitcast.84, f32[8,128,128]{2,1,0:T(8,128)} %get-tuple-element.109.cx_ref, f32[8,128,128]{2,1,0:T(8,128)} %get-tuple-element.108.cy_ref, f32[8,128,128]{2,1,0:T(8,128)} %get-tuple-element.107.cz_ref, f32[8,128,128]{2,1,0:T(8,128)} %get-tuple-element.106.inv_ref), custom_call_target="tpu_custom_call" | custom-call | tf_op jit(solution)/shard_map/pallas_call | solution.py:138
  118.6 1.2 fusion.4
  119.8 0.3 fusion.2
  120.1 18.1 %all-gather = f32[64,1,128]{2,0,1:T(8,128)S(1)} all-gather(f32[8,1,128]{2,0,1:T(8,128)S(1)} %slice.117), channel_id=2, replica_groups=mesh['plan'=32,'draw'=8] {'draw'}, dimensions={0}, use_global_device_ids=true | all-gather | bytes 36864 | tf_op jit(solution)/shard_map/all_gather | solution.py:26
  138.2 0.0 copy-done.2
  138.2 0.2 copy.32
  138.4 0.4 bitcast_multiply_fusion
  138.9 0.0 copy-start
  138.9 23.3 %fusion.18 = f32[8,128,128]{2,0,1:T(8,128)S(1)} fusion(f32[8,128,128]{2,0,1:T(8,128)S(1)} %rev.7), kind=kOutput, calls=%fused_computation.63 | output fusion | flops 16646144 | bytes 1048576 | tf_op jit(solution)/shard_map/jit(cumsum)/reduce_window_sum | solution.py:170
  162.2 0.1 copy.33
  162.4 0.2 rev.8
  162.6 18.3 %all-gather.1 = f32[64,1,128]{2,0,1:T(8,128)S(1)} all-gather(f32[8,1,128]{2,0,1:T(8,128)S(1)} %slice.118), channel_id=3, replica_groups=mesh['plan'=32,'draw'=8] {'draw'}, dimensions={0}, use_global_device_ids=true | all-gather | bytes 36864 | tf_op jit(solution)/shard_map/all_gather | solution.py:26
  180.9 0.2 while.23
  181.1 0.0 copy-done
  181.1 1.1 multiply_multiply_fusion.src_ref
  182.2 81.5 %shard_map.77 = f32[8,128,128]{2,1,0:T(8,128)} custom-call(f32[8,128,128]{2,1,0:T(8,128)} %multiply_multiply_fusion.src_ref, f32[8,128,128]{2,1,0:T(8,128)} %get-tuple-element.109.cx_ref, f32[8,128,128]{2,1,0:T(8,128)} %get-tuple-element.108.cy_ref, f32[8,128,128]{2,1,0:T(8,128)} %get-tuple-element.107.cz_ref, f32[8,128,128]{2,1,0:T(8,128)} %get-tuple-element.106.inv_ref), custom_call_target="tpu_custom_call" | custom-call | tf_op jit(solution)/shard_map/pallas_call | solution.py:138
  263.7 1.2 copy.38
  264.9 0.0 copy-start.3
  264.9 4.5 %scatter_custom_fusion.1 = f32[4096,128]{1,0:T(8,128)} fusion(s32[1024]{0:T(1024)S(1)} %bitcast.96, f32[1024,128]{1,0:T(8,128)S(1)} %bitcast.86, f32[]{:T(128)} %constant.101.clone.1), kind=kCustom, calls=%fused_computation.5 | custom fusion | bytes 2097156 | tf_op jit(solution)/shard_map/scatter | solution.py:198
  269.5 0.0 all-to-all-done
  269.5 0.0 copy-done.3
  269.5 17.4 %all-to-all-start.1 = ((f32[32,128,128]{2,1,0:T(8,128)}), f32[32,128,128]{2,1,0:T(8,128)S(1)}, u32[]{:S(2)}, u32[]{:S(2)}) async-start(f32[32,128,128]{2,1,0:T(8,128)} %bitcast.45), calls=%async_computation.1 | async-start | bytes 4194304 | tf_op jit(solution)/shard_map/all_to_all | solution.py:205
  286.9 1.0 copy.37
  287.9 27.2 %all-to-all-done.1 = f32[32,128,128]{2,1,0:T(8,128)S(1)} async-done(((f32[32,128,128]{2,1,0:T(8,128)}), f32[32,128,128]{2,1,0:T(8,128)S(1)}, u32[]{:S(2)}, u32[]{:S(2)}) %all-to-all-start.1) | async-done | bytes 2097184 | tf_op jit(solution)/shard_map/all_to_all | solution.py:205
  315.2 26.7 %scatter_custom_fusion.2 = f32[513,128]{1,0:T(8,128)S(1)} fusion(s32[4096]{0:T(1024)S(1)} %bitcast.94, f32[4096,128]{1,0:T(8,128)S(1)} %bitcast.83, f32[]{:T(128)} %constant.101.clone.1), kind=kCustom, calls=%fused_computation.28 | custom fusion | flops 524288 | bytes 262660 | tf_op jit(solution)/shard_map/scatter-add | solution.py:212
  341.9 0.7 slice_multiply_fusion
  (19 shorter events, 0.2 us)
Async XLA Ops:
  0.6 30.8 %copy-start.1 = (f32[8,128,128]{2,1,0:T(8,128)S(1)}, f32[8,128,128]{2,1,0:T(8,128)}, u32[]{:S(2)}) copy-start(f32[8,128,128]{2,1,0:T(8,128)} %param.9) | copy-start | bytes 1572868
  17.2 252.2 %all-to-all-start = ((f32[32,1,128]{2,1,0:T(1,128)}), f32[32,1,128]{2,1,0:T(1,128)S(1)}, u32[]{:S(2)}, u32[]{:S(2)}) async-start(f32[32,1,128]{2,1,0:T(1,128)} %bitcast.42), calls=%async_computation | async-start | bytes 32768 | tf_op jit(solution)/shard_map/all_to_all | solution.py:208
  49.8 88.4 %copy-start.2 = (f32[8,128,128]{2,1,0:T(8,128)S(1)}, f32[8,128,128]{2,1,0:T(8,128)}, u32[]{:S(2)}) copy-start(f32[8,128,128]{2,1,0:T(8,128)} %param.12) | copy-start | bytes 1572868
  138.9 42.2 %copy-start = (f32[8,128,128]{2,1,0:T(8,128)S(1)}, f32[8,128,128]{2,1,0:T(8,128)}, u32[]{:S(2)}) copy-start(f32[8,128,128]{2,1,0:T(8,128)} %shard_map.76) | copy-start | bytes 1572868
  264.9 4.5 %copy-start.3 = (f32[8,128,128]{2,1,0:T(8,128)}, f32[8,128,128]{2,1,0:T(8,128)S(1)}, u32[]{:S(2)}) copy-start(f32[8,128,128]{2,1,0:T(8,128)S(1)} %copy.38) | copy-start | bytes 1572868
  269.5 45.7 %all-to-all-start.1 = ((f32[32,128,128]{2,1,0:T(8,128)}), f32[32,128,128]{2,1,0:T(8,128)S(1)}, u32[]{:S(2)}, u32[]{:S(2)}) async-start(f32[32,128,128]{2,1,0:T(8,128)} %bitcast.45), calls=%async_computation.1 | async-start | bytes 4194304 | tf_op jit(solution)/shard_map/all_to_all | solution.py:205

commit v2 on v1

--- a/solution.py
+++ b/solution.py
@@ -19,34 +19,82 @@
 MESH = pl.DeviceIdType.MESH
 
 
-def entering(part, axis, combine, identity, reverse):
-    count = lax.axis_size(axis)
-    place = lax.axis_index(axis)
-    ahead = count - 1 - place if reverse else place
-    gathered = lax.all_gather(part, axis)
-    state = jnp.zeros_like(part) + jnp.asarray(identity, part.dtype)
-
-    def one(step, state):
-        source = count - 1 - step if reverse else step
-        return combine(state, lax.dynamic_index_in_dim(gathered, source, 0, False))
-
-    return lax.fori_loop(0, ahead, one, state)
-
-
-def coefficients(class_ids, class_radii):
-    coef_x = jnp.zeros(class_ids.shape, jnp.float32)
-    coef_y = jnp.zeros(class_ids.shape, jnp.float32)
-    coef_z = jnp.zeros(class_ids.shape, jnp.float32)
-    for level in range(class_radii.shape[0]):
-        hit = class_ids == level
-        coef_x = jnp.where(hit, class_radii[level, 0], coef_x)
-        coef_y = jnp.where(hit, class_radii[level, 1], coef_y)
-        coef_z = jnp.where(hit, class_radii[level, 2], coef_z)
-    return (coef_x, coef_y, coef_z)
-
-
-def filter_kernel(n_plan, n_draw, src_ref, cx_ref, cy_ref, cz_ref, inv_ref, out_ref, field, send_sem, recv_sem):
+def scan_kernel(n_draw, reverse, part_ref, out_ref, held, send_sem, recv_sem):
+    p = lax.axis_index("plan")
+    d = lax.axis_index("draw")
+    held[...] = jnp.zeros_like(held)
+    barrier = pltpu.get_barrier_semaphore()
+    for e in range(n_draw):
+        @pl.when(d != e)
+        def _():
+            pl.semaphore_signal(barrier, 1, device_id=(p, e), device_id_type=MESH)
+    pl.semaphore_wait(barrier, n_draw - 1)
+
+    def later(e):
+        return e < d if reverse else e > d
+
+    def earlier(e):
+        return e > d if reverse else e < d
+
+    sends = []
+    for e in range(n_draw):
+        copy = pltpu.make_async_remote_copy(
+            part_ref, held.at[d], send_sem.at[e], recv_sem.at[d], device_id=(p, e), device_id_type=MESH)
+        sends.append(copy)
+
+        @pl.when(later(e))
+        def _():
+            copy.start()
+    for e in range(n_draw):
+        incoming = pltpu.make_async_remote_copy(
+            part_ref, held.at[e], send_sem.at[e], recv_sem.at[e], device_id=(p, e), device_id_type=MESH)
+
+        @pl.when(later(e))
+        def _():
+            sends[e].wait_send()
+
+        @pl.when(earlier(e))
+        def _():
+            incoming.wait_recv()
+    total = held[0]
+    for e in range(1, n_draw):
+        total = total + held[e]
+    out_ref[...] = total
+
+
+def entering(part, n_draw, reverse, kid):
+    vmem = pl.BlockSpec(memory_space=pltpu.VMEM)
+    return pl.pallas_call(
+        functools.partial(scan_kernel, n_draw, reverse),
+        out_shape=jax.ShapeDtypeStruct(part.shape, jnp.float32),
+        in_specs=[vmem],
+        out_specs=vmem,
+        scratch_shapes=[
+            pltpu.VMEM((n_draw,) + part.shape, jnp.float32),
+            pltpu.SemaphoreType.DMA((n_draw,)),
+            pltpu.SemaphoreType.DMA((n_draw,)),
+        ],
+        compiler_params=pltpu.CompilerParams(collective_id=kid, has_side_effects=True),
+    )(part)
+
+
+def filter_kernel(n_plan, n_draw, src_ref, ids_ref, radii_ref, out_ref, field, cx_ref, cy_ref, cz_ref, inv_ref,
+                  send_sem, recv_sem):
     planes, depth, width = src_ref.shape
+    for i in range(planes):
+        cls = ids_ref[i]
+        cx = jnp.zeros((depth, width), jnp.float32)
+        cy = jnp.zeros((depth, width), jnp.float32)
+        cz = jnp.zeros((depth, width), jnp.float32)
+        for level in range(radii_ref.shape[0]):
+            hit = cls == level
+            cx = jnp.where(hit, radii_ref[level, 0], cx)
+            cy = jnp.where(hit, radii_ref[level, 1], cy)
+            cz = jnp.where(hit, radii_ref[level, 2], cz)
+        cx_ref[i] = cx
+        cy_ref[i] = cy
+        cz_ref[i] = cz
+        inv_ref[i] = 1.0 / (1.0 + 2.0 * (cx + cy + cz))
     p = lax.axis_index("plan")
     d = lax.axis_index("draw")
     has_l = p > 0
@@ -132,46 +180,45 @@
     sweep(1, True)
 
 
-def smooth_each(source, coef_x, coef_y, coef_z, inv_diag, n_plan, n_draw, kid):
+def smooth_each(source, class_ids, class_radii, n_plan, n_draw, kid):
     planes, depth, width = source.shape
     vmem = pl.BlockSpec(memory_space=pltpu.VMEM)
+    smem = pl.BlockSpec(memory_space=pltpu.SMEM)
     return pl.pallas_call(
         functools.partial(filter_kernel, n_plan, n_draw),
         out_shape=jax.ShapeDtypeStruct(source.shape, jnp.float32),
-        in_specs=[vmem] * 5,
+        in_specs=[vmem, vmem, smem],
         out_specs=vmem,
         scratch_shapes=[
             pltpu.VMEM((2, planes + 2, depth + 2 * HALO, width), jnp.float32),
+            pltpu.VMEM(source.shape, jnp.float32),
+            pltpu.VMEM(source.shape, jnp.float32),
+            pltpu.VMEM(source.shape, jnp.float32),
+            pltpu.VMEM(source.shape, jnp.float32),
             pltpu.SemaphoreType.DMA((2, 4)),
             pltpu.SemaphoreType.DMA((2, 4)),
         ],
         compiler_params=pltpu.CompilerParams(collective_id=kid, has_side_effects=True),
-    )(source, coef_x, coef_y, coef_z, inv_diag)
+    )(source, class_ids, class_radii)
 
 
 def per_device(n_plan, n_draw, design, class_ids, class_radii, sensitivity, row_patch):
     design_t = jnp.swapaxes(design, 1, 2)
     ids_t = jnp.swapaxes(class_ids, 1, 2)
     sens_t = jnp.swapaxes(sensitivity, 1, 2)
-    coef_x, coef_y, coef_z = coefficients(ids_t, class_radii)
-    inv_diag = 1.0 / (1.0 + 2.0 * (coef_x + coef_y + coef_z))
-    filtered = smooth_each(design_t, coef_x, coef_y, coef_z, inv_diag, n_plan, n_draw, 0)
+    filtered = smooth_each(design_t, ids_t, class_radii, n_plan, n_draw, 0)
     denom = jnp.tanh(jnp.float32(BETA * ETA)) + jnp.tanh(jnp.float32(BETA * (1.0 - ETA)))
     steep = jnp.tanh(BETA * (filtered - ETA))
     projected = RMIN + (1.0 - RMIN) * (jnp.tanh(jnp.float32(BETA * ETA)) + steep) / denom
     running = jnp.cumsum(jnp.power(projected, POWER), axis=1)
     totals = running[:, -1, :]
-    carried = entering(
-        totals, "draw", lambda first, second: first + second, jnp.zeros_like(totals), False
-    )
+    carried = entering(totals, n_draw, False, 2)
     prefix = running + carried[:, None, :]
     cast_density = jnp.power(prefix, 1.0 / POWER)
     weighted = sens_t * jnp.power(prefix, (1.0 - POWER) / POWER)
-    backward = jnp.flip(jnp.cumsum(jnp.flip(weighted, 1), axis=1), 1)
+    backward = lax.cumsum(weighted, axis=1, reverse=True)
     rests = backward[:, 0, :]
-    below = entering(
-        rests, "draw", lambda first, second: first + second, jnp.zeros_like(rests), True
-    )
+    below = entering(rests, n_draw, True, 3)
     suffix = backward + below[:, None, :]
     chained = (
         jnp.power(projected, POWER - 1.0)
@@ -181,7 +228,7 @@
         * (1.0 - steep * steep)
         / denom
     )
-    filtered_sens_t = smooth_each(chained, coef_x, coef_y, coef_z, inv_diag, n_plan, n_draw, 1)
+    filtered_sens_t = smooth_each(chained, ids_t, class_radii, n_plan, n_draw, 1)
     filtered_sens = jnp.swapaxes(filtered_sens_t, 1, 2)
     cast_density = jnp.swapaxes(cast_density, 1, 2)
     depth = filtered_sens.shape[2]
@@ -192,15 +239,17 @@
     patch_ids = row_patch.reshape(row_count)
     owners = patch_ids // PATCH_DEV
     slot_patch = patch_ids - owners * PATCH_DEV
-    onehot = (owners[:, None] == jnp.arange(tiles, dtype=jnp.int32)[None, :]).astype(jnp.int32)
-    ranking = jnp.sum(jnp.cumsum(onehot, axis=0) * onehot, axis=1) - 1
+    onehot = (owners[:, None] == jnp.arange(tiles, dtype=jnp.int32)[None, :]).astype(jnp.bfloat16)
+    rows = jnp.arange(row_count, dtype=jnp.int32)
+    upto = (rows[None, :] <= rows[:, None]).astype(jnp.bfloat16)
+    counted = jnp.dot(upto, onehot, preferred_element_type=jnp.float32)
+    ranking = jnp.sum(counted * onehot.astype(jnp.float32), axis=1).astype(jnp.int32) - 1
     position = owners * capacity + ranking
-    sendbuf = jnp.zeros((tiles * capacity, depth), jnp.float32).at[position].set(row_data)
-    send_ids = (
-        jnp.full((tiles * capacity,), float(PATCH_DEV), jnp.float32)
-        .at[position]
-        .set(slot_patch.astype(jnp.float32))
-    )
+    source_row = jnp.full((tiles * capacity,), row_count, jnp.int32).at[position].set(rows)
+    padded_rows = jnp.concatenate([row_data, jnp.zeros((1, depth), jnp.float32)], axis=0)
+    padded_ids = jnp.concatenate([slot_patch.astype(jnp.float32), jnp.full((1,), float(PATCH_DEV), jnp.float32)])
+    sendbuf = jnp.take(padded_rows, source_row, axis=0)
+    send_ids = jnp.take(padded_ids, source_row, axis=0)
     arrived, arrived_ids = (
         lax.all_to_all(
             sendbuf.reshape(tiles, capacity, depth), "plan", split_axis=0, concat_axis=0, tiled=True
@@ -209,12 +258,12 @@
             send_ids.reshape(tiles, capacity), "plan", split_axis=0, concat_axis=0, tiled=True
         ),
     )
-    summed = jax.ops.segment_sum(
-        arrived.reshape(tiles * capacity, depth),
-        arrived_ids.reshape(tiles * capacity).astype(jnp.int32),
-        num_segments=PATCH_DEV + 1,
-    )
-    patch_sens = 0.25 * summed[:PATCH_DEV]
+    picks = (
+        jnp.arange(PATCH_DEV, dtype=jnp.int32)[:, None] == arrived_ids.reshape(1, tiles * capacity).astype(jnp.int32)
+    ).astype(jnp.float32)
+    summed = jnp.dot(picks, arrived.reshape(tiles * capacity, depth), precision=lax.Precision.HIGHEST,
+                     preferred_element_type=jnp.float32)
+    patch_sens = 0.25 * summed
     return (cast_density, filtered_sens, patch_sens)
 
 

time: 343 us -> 270 us (0.79)
  other arithmetic: 83.3 us -> 9.4 us
  blocking collectives: 36.4 us -> 0 us
  local copies, waits for them, and re-layouts: 18.4 us -> 45.3 us
  Pallas kernels: 150 us -> 156 us
  matrix products: 0 us -> 5.32 us
    all_gather x2 -> x0, blocking collectives: 36.4 us -> none  [entering(): gathered = lax.all_gather(part, axis)]
    gather x0 -> x2, local copies, waits for them, and re-layouts: none -> 33.8 us  [the longest x1 23 us: per_device(): send_ids = jnp.take(padded_ids, source_row, axis=0)]
    another operation x4 -> x1, other arithmetic: 32.5 us -> 2.04 us  [per_device(): backward = lax.cumsum(weighted, axis=1, reverse=True)]
    scatter-add x1 -> x0, other arithmetic: 26.7 us -> none  [per_device(): jax.ops.segment_sum(arrived.reshape(tiles * capacity, depth), arrived_ids...]
    div x1 -> x0, other arithmetic: 17.4 us -> none  [per_device(): inv_diag = 1.0 / (1.0 + 2.0 * (coef_x + coef_y + coef_z))]
    pallas_call x0 -> x2, Pallas kernels: none -> 15.7 us  [entering(): pl.pallas_call(functools.partial(scan_kernel, n_draw, reverse), out_shape...]
    pallas_call x2, Pallas kernels: 150 us -> 140 us  [smooth_each(): pl.pallas_call(functools.partial(filter_kernel, n_plan, n_draw), out_shap...]
    dot_general x0 -> x2, matrix products: none -> 5.32 us  [the longest x1 4.78 us: per_device(): jnp.dot(picks, arrived.reshape(tiles * capacity, depth), precision=lax.Pr...]
  transfers between devices with their start and end apart: 2 -> 2, of which waited for: 1 -> 1; matrix products, arithmetic and copies ran while one was open for 17% -> 9% of each run, Pallas kernels for 44% -> 58%
where the time goes in v2:
time: 270 us
  Pallas kernels  156 us (58%)
  local copies, waits for them, and re-layouts  45.3 us (17%)
  waiting for transfers between devices  27 us (10%)
  starting transfers between devices  26.1 us (10%)
  other arithmetic  9.4 us (3%)
  matrix products  5.32 us (2%)
    pallas_call x2, Pallas kernels, smooth_each(): pl.pallas_call(functools.partial(filter_kernel, n_plan, n_draw), out_shap...  140 us
    all_to_all x1, waiting for transfers between devices, per_device(): lax.all_to_all(sendbuf.reshape(tiles, capacity, depth), 'plan', split_axi...  27 us
    gather x1, local copies, waits for them, and re-layouts, per_device(): send_ids = jnp.take(padded_ids, source_row, axis=0)  23 us
    all_to_all x1, starting transfers between devices, per_device(): lax.all_to_all(sendbuf.reshape(tiles, capacity, depth), 'plan', split_axi...  17.6 us
    pallas_call x2, Pallas kernels, entering(): pl.pallas_call(functools.partial(scan_kernel, n_draw, reverse), out_shape...  15.7 us
    gather x1, local copies, waits for them, and re-layouts, per_device(): sendbuf = jnp.take(padded_rows, source_row, axis=0)  10.8 us
    all_to_all x1, starting transfers between devices, per_device(): lax.all_to_all(send_ids.reshape(tiles, capacity), 'plan', split_axis=0, c...  8.59 us
    unnamed x20, local copies, waits for them, and re-layouts  5.98 us
  transfers between devices with their start and end apart: 2, of which 1 were waited for; matrix products, arithmetic and copies ran while one was open for 9% of the time, Pallas kernels for 58%

profile of v2, /device:TPU:1, one launch (start us, length us, event | category | flops | bytes accessed | tf_op | source)
XLA Modules:
  0.0 269.9 jit_solution(16906931706313361020)
XLA Ops:
  0.6 0.7 subtract_convert_fusion
  1.3 0.5 fusion.5
  1.9 0.7 compare_select_fusion.1
  2.6 4.3 %scatter_custom_fusion = s32[4096]{0:T(1024)S(1)} fusion(s32[1024]{0:T(1024)S(1)} %bitcast.44, s32[1024]{0:T(1024)S(1)} %iota.17, s32[]{:T(128)} %constant.80.clone.1), kind=kCustom, calls=%fused_computation.42 | custom fusion | bytes 16388 | tf_op jit(solution)/shard_map/scatter | solution.py:248
  7.0 0.0 copy-start.6
  7.0 0.0 copy-start.2
  7.0 0.0 copy-start.3
  7.0 23.0 %gather_fusion = f32[4096]{0:T(1024)S(1)} fusion(f32[1025]{0:T(1024)S(1)} %pad_maximum_fusion, s32[4096]{0:T(1024)S(1)} %fusion.20), kind=kCustom, calls=%fused_computation | custom fusion | bytes 49152 | tf_op jit(solution)/shard_map/jit(_take)/gather | solution.py:252
  30.1 0.6 broadcast_select_fusion.1
  30.7 8.6 %all-to-all-start = ((f32[32,1,128]{2,1,0:T(1,128)}), f32[32,1,128]{2,1,0:T(1,128)S(1)}, u32[]{:S(2)}, u32[]{:S(2)}) async-start(f32[32,1,128]{2,1,0:T(1,128)} %bitcast.11), calls=%async_computation | async-start | bytes 32768 | tf_op jit(solution)/shard_map/all_to_all | solution.py:257
  39.3 0.0 copy-done.6
  39.3 0.7 copy.19.radii_ref
  39.9 0.0 copy-done.2
  40.0 1.0 copy.17
  40.9 0.0 copy-done.3
  41.0 1.0 copy.18
  41.9 0.0 copy-start.4
  41.9 69.1 %shard_map.76 = f32[8,128,128]{2,1,0:T(8,128)} custom-call(f32[8,128,128]{2,1,0:T(8,128)} %bitcast.37, s32[8,128,128]{2,1,0:T(8,128)} %bitcast.34, f32[8,3]{1,0:T(8,128)} %copy.19.radii_ref), custom_call_target="tpu_custom_call" | custom-call | tf_op jit(solution)/shard_map/pallas_call | solution.py:187
  111.1 1.2 fusion.14
  112.3 0.0 copy-start
  112.3 0.3 fusion.11
  112.6 0.6 slice_bitcast_fusion.1.part_ref
  113.2 6.8 %shard_map.77 = f32[8,128]{1,0:T(8,128)} custom-call(f32[8,128]{1,0:T(8,128)} %slice_bitcast_fusion.1.part_ref), custom_call_target="tpu_custom_call" | custom-call | tf_op jit(solution)/shard_map/pallas_call | solution.py:67
  120.0 0.0 copy-done.4
  120.0 0.2 copy.21
  120.3 2.0 fusion.6
  122.3 0.6 slice_bitcast_fusion.part_ref
  122.9 8.9 %shard_map.78 = f32[8,128]{1,0:T(8,128)} custom-call(f32[8,128]{1,0:T(8,128)} %slice_bitcast_fusion.part_ref), custom_call_target="tpu_custom_call" | custom-call | tf_op jit(solution)/shard_map/pallas_call | solution.py:67
  131.8 0.0 copy-done
  131.8 1.8 fusion.10.src_ref
  133.6 71.1 %shard_map.79 = f32[8,128,128]{2,1,0:T(8,128)} custom-call(f32[8,128,128]{2,1,0:T(8,128)} %fusion.10.src_ref, s32[8,128,128]{2,1,0:T(8,128)} %bitcast.35, f32[8,3]{1,0:T(8,128)} %copy.19.radii_ref), custom_call_target="tpu_custom_call" | custom-call | tf_op jit(solution)/shard_map/pallas_call | solution.py:187
  204.7 1.2 copy.26
  205.9 0.0 copy-start.1
  205.9 0.8 copy-done.1
  206.7 10.8 %gather_fusion.1 = f32[4096,128]{1,0:T(8,128)S(1)} fusion(f32[1025,128]{1,0:T(8,128)S(1)} %concatenate.7, s32[4096]{0:T(1024)S(1)} %fusion.20), kind=kCustom, calls=%fused_computation.1 | custom fusion | bytes 4210688 | tf_op jit(solution)/shard_map/jit(_take)/gather | solution.py:251
  217.5 1.7 broadcast_select_fusion
  219.2 0.0 copy-start.5
  219.2 0.0 all-to-all-done
  219.2 17.6 %all-to-all-start.1 = ((f32[32,128,128]{2,1,0:T(8,128)}), f32[32,128,128]{2,1,0:T(8,128)S(1)}, u32[]{:S(2)}, u32[]{:S(2)}) async-start(f32[32,128,128]{2,1,0:T(8,128)} %broadcast_select_fusion), calls=%async_computation.1 | async-start | bytes 4194304 | tf_op jit(solution)/shard_map/all_to_all | solution.py:254
  236.8 0.0 copy-done.5
  236.8 0.3 power_bitcast_fusion
  237.1 1.0 copy.25
  238.1 27.0 %all-to-all-done.1 = f32[32,128,128]{2,1,0:T(8,128)S(1)} async-done(((f32[32,128,128]{2,1,0:T(8,128)}), f32[32,128,128]{2,1,0:T(8,128)S(1)}, u32[]{:S(2)}, u32[]{:S(2)}) %all-to-all-start.1) | async-done | bytes 2097184 | tf_op jit(solution)/shard_map/all_to_all | solution.py:254
  265.1 4.8 %fusion.3 = f32[512,128]{1,0:T(8,128)} fusion(f32[4096,128]{1,0:T(8,128)S(1)} %bitcast.38, s32[4096]{0:T(1024)S(1)} %bitcast.43), kind=kOutput, calls=%fused_computation.8 | convolution fusion | flops 3223388160 | bytes 2375680 | tf_op jit(solution)/shard_map/dot_general | solution.py:264
  (6 shorter events, 0.1 us)
Async XLA Ops:
  7.0 32.3 %copy-start.6 = (f32[8,3]{0,1:T(4,128)S(1)}, f32[8,3]{0,1:T(4,128)}, u32[]{:S(2)}) copy-start(f32[8,3]{0,1:T(4,128)} %param.7) | copy-start | bytes 292
  7.0 33.0 %copy-start.2 = (f32[8,128,128]{2,1,0:T(8,128)S(1)}, f32[8,128,128]{2,1,0:T(8,128)}, u32[]{:S(2)}) copy-start(f32[8,128,128]{2,1,0:T(8,128)} %param.5) | copy-start | bytes 1572868
  7.0 33.9 %copy-start.3 = (s32[8,128,128]{2,1,0:T(8,128)S(1)}, s32[8,128,128]{2,1,0:T(8,128)}, u32[]{:S(2)}) copy-start(s32[8,128,128]{2,1,0:T(8,128)} %param.6) | copy-start | bytes 1572868
  30.7 188.6 %all-to-all-start = ((f32[32,1,128]{2,1,0:T(1,128)}), f32[32,1,128]{2,1,0:T(1,128)S(1)}, u32[]{:S(2)}, u32[]{:S(2)}) async-start(f32[32,1,128]{2,1,0:T(1,128)} %bitcast.11), calls=%async_computation | async-start | bytes 32768 | tf_op jit(solution)/shard_map/all_to_all | solution.py:257
  41.9 78.1 %copy-start.4 = (f32[8,128,128]{2,1,0:T(8,128)S(1)}, f32[8,128,128]{2,1,0:T(8,128)}, u32[]{:S(2)}) copy-start(f32[8,128,128]{2,1,0:T(8,128)} %param.8) | copy-start | bytes 1572868
  112.3 19.5 %copy-start = (f32[8,128,128]{2,1,0:T(8,128)S(1)}, f32[8,128,128]{2,1,0:T(8,128)}, u32[]{:S(2)}) copy-start(f32[8,128,128]{2,1,0:T(8,128)} %shard_map.76) | copy-start | bytes 1572868
  205.9 0.8 copy-start.1
  219.2 17.6 %copy-start.5 = (f32[8,128]{1,0:T(8,128)S(1)}, f32[8,128]{1,0:T(8,128)}, u32[]{:S(2)}) copy-start(f32[8,128]{1,0:T(8,128)} %shard_map.77) | copy-start | bytes 12292
  219.2 45.9 %all-to-all-start.1 = ((f32[32,128,128]{2,1,0:T(8,128)}), f32[32,128,128]{2,1,0:T(8,128)S(1)}, u32[]{:S(2)}, u32[]{:S(2)}) async-start(f32[32,128,128]{2,1,0:T(8,128)} %broadcast_select_fusion), calls=%async_computation.1 | async-start | bytes 4194304 | tf_op jit(solution)/shard_map/all_to_all | solution.py:254

commit v3 on v2

--- a/solution.py
+++ b/solution.py
@@ -149,35 +149,62 @@
 
     lane = lax.broadcasted_iota(jnp.int32, (depth, width), 1)
 
-    def sweep(s, last):
+    def update(s, i, r0, rows, last):
+        at = lo + r0
+        c = field[s, i + 1, pl.ds(at, rows), :]
+        zm = field[s, i + 1, pl.ds(at - 1, rows), :]
+        zp = field[s, i + 1, pl.ds(at + 1, rows), :]
+        xm = field[s, i, pl.ds(at, rows), :]
+        xp = field[s, i + 2, pl.ds(at, rows), :]
+        lanes = lane[:rows]
+        ym = jnp.where(lanes == 0, 0.0, pltpu.roll(c, 1, 1))
+        yp = jnp.where(lanes == width - 1, 0.0, pltpu.roll(c, width - 1, 1))
+        part = pl.ds(r0, rows)
+        new = (src_ref[i, part, :] + cx_ref[i, part, :] * (xm + xp) + cy_ref[i, part, :] * (ym + yp)
+               + cz_ref[i, part, :] * (zm + zp)) * inv_ref[i, part, :]
+        if last:
+            out_ref[i, part, :] = new
+        else:
+            field[1 - s, i + 1, pl.ds(at, rows), :] = new
+
+    def sweep_send(s):
         t = 1 - s
-        for i in range(planes):
-            c = field[s, i + 1, pl.ds(lo, depth), :]
-            zm = field[s, i + 1, pl.ds(lo - 1, depth), :]
-            zp = field[s, i + 1, pl.ds(lo + 1, depth), :]
-            xm = field[s, i, pl.ds(lo, depth), :]
-            xp = field[s, i + 2, pl.ds(lo, depth), :]
-            ym = jnp.where(lane == 0, 0.0, pltpu.roll(c, 1, 1))
-            yp = jnp.where(lane == width - 1, 0.0, pltpu.roll(c, width - 1, 1))
-            new = (src_ref[i] + cx_ref[i] * (xm + xp) + cy_ref[i] * (ym + yp) + cz_ref[i] * (zm + zp)) * inv_ref[i]
-            if last:
-                out_ref[i] = new
-            else:
-                field[t, i + 1, pl.ds(lo, depth), :] = new
+        group = copies(t)
+        update(s, 0, 0, depth, False)
+        update(s, planes - 1, 0, depth, False)
+        for copy, send, _ in group[:2]:
+            @pl.when(send)
+            def _():
+                copy.start()
+        for i in range(1, planes - 1):
+            update(s, i, 0, HALO, False)
+            update(s, i, depth - HALO, HALO, False)
+        for copy, send, _ in group[2:]:
+            @pl.when(send)
+            def _():
+                copy.start()
+        for i in range(1, planes - 1):
+            update(s, i, HALO, depth - 2 * HALO, False)
+        for copy, send, recv in group:
+            @pl.when(send)
+            def _():
+                copy.wait_send()
+
+            @pl.when(recv)
+            def _():
+                copy.wait_recv()
 
     exchange(0)
 
     def pair(k, carry):
-        sweep(0, False)
-        exchange(1)
-        sweep(1, False)
-        exchange(0)
+        sweep_send(0)
+        sweep_send(1)
         return carry
 
     lax.fori_loop(0, SWEEPS // 2 - 1, pair, 0)
-    sweep(0, False)
-    exchange(1)
-    sweep(1, True)
+    sweep_send(0)
+    for i in range(planes):
+        update(1, i, 0, depth, True)
 
 
 def smooth_each(source, class_ids, class_radii, n_plan, n_draw, kid):
@@ -246,10 +273,13 @@
     ranking = jnp.sum(counted * onehot.astype(jnp.float32), axis=1).astype(jnp.int32) - 1
     position = owners * capacity + ranking
     source_row = jnp.full((tiles * capacity,), row_count, jnp.int32).at[position].set(rows)
-    padded_rows = jnp.concatenate([row_data, jnp.zeros((1, depth), jnp.float32)], axis=0)
-    padded_ids = jnp.concatenate([slot_patch.astype(jnp.float32), jnp.full((1,), float(PATCH_DEV), jnp.float32)])
-    sendbuf = jnp.take(padded_rows, source_row, axis=0)
-    send_ids = jnp.take(padded_ids, source_row, axis=0)
+    table = jnp.concatenate(
+        [row_data, jnp.broadcast_to(slot_patch.astype(jnp.float32)[:, None], (row_count, depth))], axis=1)
+    table = jnp.concatenate(
+        [table, jnp.concatenate([jnp.zeros((1, depth), jnp.float32), jnp.full((1, depth), float(PATCH_DEV))], axis=1)])
+    packed = jnp.take(table, source_row, axis=0)
+    sendbuf = packed[:, :depth]
+    send_ids = packed[:, depth]
     arrived, arrived_ids = (
         lax.all_to_all(
             sendbuf.reshape(tiles, capacity, depth), "plan", split_axis=0, concat_axis=0, tiled=True

time: 270 us -> 256 us (0.948)
  local copies, waits for them, and re-layouts: 45.3 us -> 34.9 us
  Pallas kernels: 156 us -> 151 us
  starting transfers between devices: 26.1 us -> 21.9 us
  waiting for transfers between devices: 27 us -> 30.9 us
    gather x2 -> x1, local copies, waits for them, and re-layouts: 33.8 us -> 16.1 us  [per_device(): packed = jnp.take(table, source_row, axis=0)]
    all_to_all x1, starting transfers between devices: 17.6 us -> 4.45 us  [per_device(): lax.all_to_all(sendbuf.reshape(tiles, capacity, depth), 'plan', split_axi...]
    all_to_all x1, starting transfers between devices: 8.59 us -> 17.4 us  [per_device(): lax.all_to_all(send_ids.reshape(tiles, capacity), 'plan', split_axis=0, c...]
    pallas_call x2, Pallas kernels: 140 us -> 135 us  [smooth_each(): pl.pallas_call(functools.partial(filter_kernel, n_plan, n_draw), out_shap...]
    slice x0 -> x2, local copies, waits for them, and re-layouts: none -> 4.28 us  [the longest x1 3.06 us: per_device(): sendbuf = packed[:, :depth]]
    all_to_all x1, waiting for transfers between devices: 0.01 us -> 3.81 us  [per_device(): lax.all_to_all(send_ids.reshape(tiles, capacity), 'plan', split_axis=0, c...]
    unnamed x20, local copies, waits for them, and re-layouts: 5.98 us -> 8.82 us
  transfers between devices with their start and end apart: 2 -> 2, of which waited for: 1 -> 2; matrix products, arithmetic and copies ran while one was open for 9% -> 2% of each run, Pallas kernels for 58% -> 0%
where the time goes in v3:
time: 256 us
  Pallas kernels  151 us (59%)
  local copies, waits for them, and re-layouts  34.9 us (14%)
  waiting for transfers between devices  30.9 us (12%)
  starting transfers between devices  21.9 us (9%)
  other arithmetic  11.3 us (4%)
  matrix products  5.32 us (2%)
    pallas_call x2, Pallas kernels, smooth_each(): pl.pallas_call(functools.partial(filter_kernel, n_plan, n_draw), out_shap...  135 us
    all_to_all x1, waiting for transfers between devices, per_device(): lax.all_to_all(sendbuf.reshape(tiles, capacity, depth), 'plan', split_axi...  27 us
    all_to_all x1, starting transfers between devices, per_device(): lax.all_to_all(send_ids.reshape(tiles, capacity), 'plan', split_axis=0, c...  17.4 us
    gather x1, local copies, waits for them, and re-layouts, per_device(): packed = jnp.take(table, source_row, axis=0)  16.1 us
    pallas_call x2, Pallas kernels, entering(): pl.pallas_call(functools.partial(scan_kernel, n_draw, reverse), out_shape...  15.7 us
    unnamed x20, local copies, waits for them, and re-layouts  8.82 us
  transfers between devices with their start and end apart: 2, of which 2 were waited for; matrix products, arithmetic and copies ran while one was open for 2% of the time, Pallas kernels for 0%

profile of v3, /device:TPU:1, one launch (start us, length us, event | category | flops | bytes accessed | tf_op | source)
XLA Modules:
  0.0 255.7 jit_solution(14582729500693109399)
XLA Ops:
  0.6 0.0 copy-start.3
  0.6 0.8 add_select_fusion
  1.4 0.5 fusion.5
  2.0 0.7 compare_select_fusion.1
  2.7 4.3 %scatter_custom_fusion = s32[4096]{0:T(1024)S(1)} fusion(s32[1024]{0:T(1024)S(1)} %bitcast.43, s32[1024]{0:T(1024)S(1)} %iota.17, s32[]{:T(128)} %constant.67.clone.1), kind=kCustom, calls=%fused_computation.41 | custom fusion | bytes 16388 | tf_op jit(solution)/shard_map/scatter | solution.py:275
  7.1 1.4 copy.29.radii_ref
  8.4 2.0 copy.27
  10.4 0.0 copy-done.3
  10.4 1.0 copy.28
  11.4 0.0 copy-start.4
  11.4 68.3 %shard_map.76 = f32[8,128,128]{2,1,0:T(8,128)} custom-call(f32[8,128,128]{2,1,0:T(8,128)} %bitcast.37, s32[8,128,128]{2,1,0:T(8,128)} %bitcast.34, f32[8,3]{1,0:T(8,128)} %copy.29.radii_ref), custom_call_target="tpu_custom_call" | custom-call | tf_op jit(solution)/shard_map/pallas_call | solution.py:214
  79.8 1.2 fusion.14
  81.0 0.0 copy-start.1
  81.0 0.3 fusion.11
  81.3 0.6 slice_bitcast_fusion.1.part_ref
  81.9 6.8 %shard_map.77 = f32[8,128]{1,0:T(8,128)} custom-call(f32[8,128]{1,0:T(8,128)} %slice_bitcast_fusion.1.part_ref), custom_call_target="tpu_custom_call" | custom-call | tf_op jit(solution)/shard_map/pallas_call | solution.py:67
  88.7 0.0 copy-done.4
  88.7 0.2 copy.31
  89.0 2.1 fusion.6
  91.0 0.6 slice_bitcast_fusion.part_ref
  91.6 8.9 %shard_map.78 = f32[8,128]{1,0:T(8,128)} custom-call(f32[8,128]{1,0:T(8,128)} %slice_bitcast_fusion.part_ref), custom_call_target="tpu_custom_call" | custom-call | tf_op jit(solution)/shard_map/pallas_call | solution.py:67
  100.5 0.0 copy-done.1
  100.5 0.0 copy-start.6
  100.5 1.8 fusion.10.src_ref
  102.3 66.6 %shard_map.79 = f32[8,128,128]{2,1,0:T(8,128)} custom-call(f32[8,128,128]{2,1,0:T(8,128)} %fusion.10.src_ref, s32[8,128,128]{2,1,0:T(8,128)} %bitcast.35, f32[8,3]{1,0:T(8,128)} %copy.29.radii_ref), custom_call_target="tpu_custom_call" | custom-call | tf_op jit(solution)/shard_map/pallas_call | solution.py:214
  168.9 1.2 copy.37
  170.1 0.0 copy-start.2
  170.1 0.2 broadcast_in_dim.18
  170.3 0.0 copy-done.6
  170.3 0.1 pad_maximum_fusion
  170.4 16.1 %gather_fusion = f32[4096,256]{1,0:T(8,128)} fusion(f32[1025,256]{1,0:T(8,128)S(1)} %pad_maximum_fusion, s32[4096]{0:T(1024)S(1)} %fusion.20), kind=kCustom, calls=%fused_computation | custom fusion | bytes 8404992 | tf_op jit(solution)/shard_map/jit(_take)/gather | solution.py:280
  186.5 0.0 copy-done.2
  186.5 4.1 %broadcast_select_fusion = f32[4096,256]{1,0:T(8,128)S(1)} fusion(f32[4096,256]{1,0:T(8,128)} %gather_fusion, pred[4096]{0:T(1024)(128)(4,1)S(1)} %compare_and_fusion), kind=kLoop, calls=%fused_computation.8 | loop fusion | flops 1048576 | bytes 8392704 | tf_op jit(solution)/shard_map/jit(_take)/select_n | solution.py:280
  190.6 0.0 copy-start
  190.6 1.9 copy-done
  192.5 1.2 slice_reduce_fusion
  193.8 17.4 %all-to-all-start = ((f32[32,1,128]{2,1,0:T(1,128)}), f32[32,1,128]{2,1,0:T(1,128)S(1)}, u32[]{:S(2)}, u32[]{:S(2)}) async-start(f32[32,1,128]{2,1,0:T(1,128)} %bitcast.12), calls=%async_computation | async-start | bytes 32768 | tf_op jit(solution)/shard_map/all_to_all | solution.py:287
  211.2 3.1 %slice.21 = f32[4096,128]{1,0:T(8,128)} slice(f32[4096,256]{1,0:T(8,128)} %copy-done), slice={[0:4096], [0:128]} | slice | bytes 4194304 | tf_op jit(solution)/shard_map/slice | solution.py:281
  214.2 3.8 %all-to-all-done = f32[32,1,128]{2,1,0:T(1,128)S(1)} async-done(((f32[32,1,128]{2,1,0:T(1,128)}), f32[32,1,128]{2,1,0:T(1,128)S(1)}, u32[]{:S(2)}, u32[]{:S(2)}) %all-to-all-start) | async-done | bytes 16416 | tf_op jit(solution)/shard_map/all_to_all | solution.py:287
  218.0 0.0 copy-start.5
  218.0 4.5 %all-to-all-start.1 = ((f32[32,128,128]{2,1,0:T(8,128)}), f32[32,128,128]{2,1,0:T(8,128)S(1)}, u32[]{:S(2)}, u32[]{:S(2)}) async-start(f32[32,128,128]{2,1,0:T(8,128)} %bitcast.14), calls=%async_computation.1 | async-start | bytes 4194304 | tf_op jit(solution)/shard_map/all_to_all | solution.py:284
  222.5 0.0 copy-done.5
  222.5 0.3 power_bitcast_fusion
  222.8 1.0 copy.36
  223.8 27.0 %all-to-all-done.1 = f32[32,128,128]{2,1,0:T(8,128)S(1)} async-done(((f32[32,128,128]{2,1,0:T(8,128)}), f32[32,128,128]{2,1,0:T(8,128)S(1)}, u32[]{:S(2)}, u32[]{:S(2)}) %all-to-all-start.1) | async-done | bytes 2097184 | tf_op jit(solution)/shard_map/all_to_all | solution.py:284
  250.9 4.8 %fusion.3 = f32[512,128]{1,0:T(8,128)} fusion(f32[4096,128]{1,0:T(8,128)S(1)} %bitcast.38, s32[4096]{0:T(1024)S(1)} %bitcast.42), kind=kOutput, calls=%fused_computation.9 | convolution fusion | flops 3223388160 | bytes 2375680 | tf_op jit(solution)/shard_map/dot_general | solution.py:294
  (5 shorter events, 0.0 us)
Async XLA Ops:
  0.6 9.8 %copy-start.3 = (s32[8,128,128]{2,1,0:T(8,128)S(1)}, s32[8,128,128]{2,1,0:T(8,128)}, u32[]{:S(2)}) copy-start(s32[8,128,128]{2,1,0:T(8,128)} %param.6) | copy-start | bytes 1572868
  11.4 77.3 %copy-start.4 = (f32[8,128,128]{2,1,0:T(8,128)S(1)}, f32[8,128,128]{2,1,0:T(8,128)}, u32[]{:S(2)}) copy-start(f32[8,128,128]{2,1,0:T(8,128)} %param.8) | copy-start | bytes 1572868
  81.0 19.5 %copy-start.1 = (f32[8,128,128]{2,1,0:T(8,128)S(1)}, f32[8,128,128]{2,1,0:T(8,128)}, u32[]{:S(2)}) copy-start(f32[8,128,128]{2,1,0:T(8,128)} %shard_map.76) | copy-start | bytes 1572868
  100.5 69.8 %copy-start.6 = (f32[1,256]{1,0:T(1,128)S(1)}, f32[1,256]{1,0:T(1,128)}, u32[]{:S(2)}) copy-start(f32[1,256]{1,0:T(1,128)} %constant.77.clone.1) | copy-start | bytes 3076
  170.1 16.4 %copy-start.2 = (f32[8,128,128]{2,1,0:T(8,128)}, f32[8,128,128]{2,1,0:T(8,128)S(1)}, u32[]{:S(2)}) copy-start(f32[8,128,128]{2,1,0:T(8,128)S(1)} %copy.37) | copy-start | bytes 1572868
  190.6 1.9 copy-start
  193.8 24.3 %all-to-all-start = ((f32[32,1,128]{2,1,0:T(1,128)}), f32[32,1,128]{2,1,0:T(1,128)S(1)}, u32[]{:S(2)}, u32[]{:S(2)}) async-start(f32[32,1,128]{2,1,0:T(1,128)} %bitcast.12), calls=%async_computation | async-start | bytes 32768 | tf_op jit(solution)/shard_map/all_to_all | solution.py:287
  218.0 4.5 %copy-start.5 = (f32[8,128]{1,0:T(8,128)S(1)}, f32[8,128]{1,0:T(8,128)}, u32[]{:S(2)}) copy-start(f32[8,128]{1,0:T(8,128)} %shard_map.77) | copy-start | bytes 12292
  218.0 32.8 %all-to-all-start.1 = ((f32[32,128,128]{2,1,0:T(8,128)}), f32[32,128,128]{2,1,0:T(8,128)S(1)}, u32[]{:S(2)}, u32[]{:S(2)}) async-start(f32[32,128,128]{2,1,0:T(8,128)} %bitcast.14), calls=%async_computation.1 | async-start | bytes 4194304 | tf_op jit(solution)/shard_map/all_to_all | solution.py:284

commit v4 on v3

--- a/solution.py
+++ b/solution.py
@@ -278,16 +278,18 @@
     table = jnp.concatenate(
         [table, jnp.concatenate([jnp.zeros((1, depth), jnp.float32), jnp.full((1, depth), float(PATCH_DEV))], axis=1)])
     packed = jnp.take(table, source_row, axis=0)
-    sendbuf = packed[:, :depth]
-    send_ids = packed[:, depth]
-    arrived, arrived_ids = (
-        lax.all_to_all(
-            sendbuf.reshape(tiles, capacity, depth), "plan", split_axis=0, concat_axis=0, tiled=True
-        ),
-        lax.all_to_all(
-            send_ids.reshape(tiles, capacity), "plan", split_axis=0, concat_axis=0, tiled=True
-        ),
+    id_rows = capacity // depth
+    sendbuf = jnp.concatenate(
+        [
+            packed[:, :depth].reshape(tiles, capacity, depth),
+            packed[:, depth].reshape(tiles, id_rows, depth),
+            jnp.zeros((tiles, (-id_rows) % 8, depth), jnp.float32),
+        ],
+        axis=1,
     )
+    arrived_all = lax.all_to_all(sendbuf, "plan", split_axis=0, concat_axis=0, tiled=True)
+    arrived = arrived_all[:, :capacity, :]
+    arrived_ids = arrived_all[:, capacity:capacity + id_rows, :]
     picks = (
         jnp.arange(PATCH_DEV, dtype=jnp.int32)[:, None] == arrived_ids.reshape(1, tiles * capacity).astype(jnp.int32)
     ).astype(jnp.float32)

time: 256 us -> 245 us (0.957)
  local copies, waits for them, and re-layouts: 34.9 us -> 29.1 us
  starting transfers between devices: 21.9 us -> 17.5 us
    all_to_all x2 -> x1, starting transfers between devices: 21.9 us -> 17.5 us  [per_device(): lax.all_to_all(sendbuf, 'plan', split_axis=0, concat_axis=0, tiled=True)]
    slice x2 -> x3, local copies, waits for them, and re-layouts: 4.28 us -> 0.99 us  [the longest x1 0.61 us: per_device(): packed[:, depth].reshape(tiles, id_rows, depth)]
    unnamed x20, local copies, waits for them, and re-layouts: 8.82 us -> 6.24 us
    all_to_all x2 -> x1, waiting for transfers between devices: 30.9 us -> 28.4 us  [per_device(): lax.all_to_all(sendbuf, 'plan', split_axis=0, concat_axis=0, tiled=True)]
  transfers between devices with their start and end apart: 2 -> 1, of which waited for: 2 -> 1; matrix products, arithmetic and copies ran while one was open for 2% -> 1% of each run, Pallas kernels for 0% -> 0%
where the time goes in v4:
time: 245 us
  Pallas kernels  151 us (62%)
  local copies, waits for them, and re-layouts  29.1 us (12%)
  waiting for transfers between devices  28.4 us (12%)
  starting transfers between devices  17.5 us (7%)
  other arithmetic  13 us (5%)
  matrix products  5.32 us (2%)
    pallas_call x2, Pallas kernels, smooth_each(): pl.pallas_call(functools.partial(filter_kernel, n_plan, n_draw), out_shap...  135 us
    all_to_all x1, waiting for transfers between devices, per_device(): lax.all_to_all(sendbuf, 'plan', split_axis=0, concat_axis=0, tiled=True)  28.4 us
    all_to_all x1, starting transfers between devices, per_device(): lax.all_to_all(sendbuf, 'plan', split_axis=0, concat_axis=0, tiled=True)  17.5 us
    gather x1, local copies, waits for them, and re-layouts, per_device(): packed = jnp.take(table, source_row, axis=0)  16.1 us
    pallas_call x2, Pallas kernels, entering(): pl.pallas_call(functools.partial(scan_kernel, n_draw, reverse), out_shape...  15.7 us
    unnamed x20, local copies, waits for them, and re-layouts  6.24 us
  transfers between devices with their start and end apart: 1, of which 1 were waited for; matrix products, arithmetic and copies ran while one was open for 1% of the time, Pallas kernels for 0%

profile of v4, /device:TPU:1, one launch (start us, length us, event | category | flops | bytes accessed | tf_op | source)
XLA Modules:
  0.0 244.7 jit_solution(1882111411503783148)
XLA Ops:
  0.6 0.0 copy-start.2
  0.6 0.0 copy-start.5
  0.7 0.8 add_select_fusion
  1.4 0.5 fusion.5
  2.0 0.7 compare_select_fusion.1
  2.7 4.3 %scatter_custom_fusion = s32[4096]{0:T(1024)S(1)} fusion(s32[1024]{0:T(1024)S(1)} %bitcast.44, s32[1024]{0:T(1024)S(1)} %iota.17, s32[]{:T(128)} %constant.68.clone.1), kind=kCustom, calls=%fused_computation.43 | custom fusion | bytes 16388 | tf_op jit(solution)/shard_map/scatter | solution.py:275
  7.1 2.0 copy.18
  9.1 0.0 copy-done.2
  9.1 0.0 copy-start.3
  9.1 1.0 copy.19
  10.1 0.0 copy-done.5
  10.1 0.7 copy.20.radii_ref
  10.8 68.3 %shard_map.76 = f32[8,128,128]{2,1,0:T(8,128)} custom-call(f32[8,128,128]{2,1,0:T(8,128)} %bitcast.37, s32[8,128,128]{2,1,0:T(8,128)} %bitcast.34, f32[8,3]{1,0:T(8,128)} %copy.20.radii_ref), custom_call_target="tpu_custom_call" | custom-call | tf_op jit(solution)/shard_map/pallas_call | solution.py:214
  79.1 0.0 copy-start
  79.1 1.3 fusion.14
  80.3 0.3 fusion.11
  80.6 0.6 slice_bitcast_fusion.1.part_ref
  81.2 6.8 %shard_map.77 = f32[8,128]{1,0:T(8,128)} custom-call(f32[8,128]{1,0:T(8,128)} %slice_bitcast_fusion.1.part_ref), custom_call_target="tpu_custom_call" | custom-call | tf_op jit(solution)/shard_map/pallas_call | solution.py:67
  88.1 0.0 copy-done.3
  88.1 0.2 copy.22
  88.3 2.1 fusion.6
  90.4 0.6 slice_bitcast_fusion.part_ref
  91.0 8.9 %shard_map.78 = f32[8,128]{1,0:T(8,128)} custom-call(f32[8,128]{1,0:T(8,128)} %slice_bitcast_fusion.part_ref), custom_call_target="tpu_custom_call" | custom-call | tf_op jit(solution)/shard_map/pallas_call | solution.py:67
  99.9 0.0 copy-done
  99.9 0.0 copy-start.6
  99.9 1.8 fusion.10.src_ref
  101.7 66.6 %shard_map.79 = f32[8,128,128]{2,1,0:T(8,128)} custom-call(f32[8,128,128]{2,1,0:T(8,128)} %fusion.10.src_ref, s32[8,128,128]{2,1,0:T(8,128)} %bitcast.35, f32[8,3]{1,0:T(8,128)} %copy.20.radii_ref), custom_call_target="tpu_custom_call" | custom-call | tf_op jit(solution)/shard_map/pallas_call | solution.py:214
  168.2 1.2 copy.28
  169.5 0.0 copy-start.1
  169.5 0.2 broadcast_in_dim.34
  169.7 0.0 copy-done.6
  169.7 0.1 pad_maximum_fusion
  169.8 16.1 %gather_fusion = f32[4096,256]{1,0:T(8,128)} fusion(f32[1025,256]{1,0:T(8,128)S(1)} %pad_maximum_fusion, s32[4096]{0:T(1024)S(1)} %fusion.20), kind=kCustom, calls=%fused_computation | custom fusion | bytes 8404992 | tf_op jit(solution)/shard_map/jit(_take)/gather | solution.py:280
  185.8 0.0 copy-done.1
  185.8 4.1 %broadcast_select_fusion = f32[4096,256]{1,0:T(8,128)S(1)} fusion(f32[4096,256]{1,0:T(8,128)} %gather_fusion, pred[4096]{0:T(1024)(128)(4,1)S(1)} %compare_and_fusion), kind=kLoop, calls=%fused_computation.9 | loop fusion | flops 1048576 | bytes 8392704 | tf_op jit(solution)/shard_map/jit(_take)/select_n | solution.py:280
  190.0 0.6 slice_reduce_fusion
  190.6 0.1 slice.28
  190.7 0.1 pad.2.clone
  190.8 1.6 maximum_maximum_fusion
  192.4 0.0 copy-start.4
  192.4 17.5 %all-to-all-start = ((f32[32,136,128]{2,1,0:T(8,128)}), f32[32,136,128]{2,1,0:T(8,128)S(1)}, u32[]{:S(2)}, u32[]{:S(2)}) async-start(f32[32,136,128]{2,1,0:T(8,128)} %maximum_maximum_fusion), calls=%async_computation | async-start | bytes 4456448 | tf_op jit(solution)/shard_map/all_to_all | solution.py:290
  210.0 0.0 copy-done.4
  210.0 0.3 power_bitcast_fusion
  210.2 1.0 copy.27
  211.3 28.4 %all-to-all-done = f32[32,136,128]{2,1,0:T(8,128)S(1)} async-done(((f32[32,136,128]{2,1,0:T(8,128)}), f32[32,136,128]{2,1,0:T(8,128)S(1)}, u32[]{:S(2)}, u32[]{:S(2)}) %all-to-all-start) | async-done | bytes 2228256 | tf_op jit(solution)/shard_map/all_to_all | solution.py:290
  239.7 0.2 slice.31
  239.9 4.8 %fusion.3 = f32[512,128]{1,0:T(8,128)} fusion(f32[4096,128]{1,0:T(8,128)S(1)} %bitcast.38, s32[4096]{0:T(1024)S(1)} %bitcast.43), kind=kOutput, calls=%fused_computation.10 | convolution fusion | flops 3223388160 | bytes 2375680 | tf_op jit(solution)/shard_map/dot_general | solution.py:296
  (6 shorter events, 0.0 us)
Async XLA Ops:
  0.6 8.5 %copy-start.2 = (s32[8,128,128]{2,1,0:T(8,128)S(1)}, s32[8,128,128]{2,1,0:T(8,128)}, u32[]{:S(2)}) copy-start(s32[8,128,128]{2,1,0:T(8,128)} %param.6) | copy-start | bytes 1572868
  0.6 9.5 %copy-start.5 = (f32[8,3]{0,1:T(4,128)S(1)}, f32[8,3]{0,1:T(4,128)}, u32[]{:S(2)}) copy-start(f32[8,3]{0,1:T(4,128)} %param.7) | copy-start | bytes 292
  9.1 79.0 %copy-start.3 = (f32[8,128,128]{2,1,0:T(8,128)S(1)}, f32[8,128,128]{2,1,0:T(8,128)}, u32[]{:S(2)}) copy-start(f32[8,128,128]{2,1,0:T(8,128)} %param.8) | copy-start | bytes 1572868
  79.1 20.8 %copy-start = (f32[8,128,128]{2,1,0:T(8,128)S(1)}, f32[8,128,128]{2,1,0:T(8,128)}, u32[]{:S(2)}) copy-start(f32[8,128,128]{2,1,0:T(8,128)} %shard_map.76) | copy-start | bytes 1572868
  99.9 69.8 %copy-start.6 = (f32[1,256]{1,0:T(1,128)S(1)}, f32[1,256]{1,0:T(1,128)}, u32[]{:S(2)}) copy-start(f32[1,256]{1,0:T(1,128)} %constant.78.clone.1) | copy-start | bytes 3076
  169.5 16.4 %copy-start.1 = (f32[8,128,128]{2,1,0:T(8,128)}, f32[8,128,128]{2,1,0:T(8,128)S(1)}, u32[]{:S(2)}) copy-start(f32[8,128,128]{2,1,0:T(8,128)S(1)} %copy.28) | copy-start | bytes 1572868
  192.4 17.5 %copy-start.4 = (f32[8,128]{1,0:T(8,128)S(1)}, f32[8,128]{1,0:T(8,128)}, u32[]{:S(2)}) copy-start(f32[8,128]{1,0:T(8,128)} %shard_map.77) | copy-start | bytes 12292
  192.4 47.3 %all-to-all-start = ((f32[32,136,128]{2,1,0:T(8,128)}), f32[32,136,128]{2,1,0:T(8,128)S(1)}, u32[]{:S(2)}, u32[]{:S(2)}) async-start(f32[32,136,128]{2,1,0:T(8,128)} %maximum_maximum_fusion), calls=%async_computation | async-start | bytes 4456448 | tf_op jit(solution)/shard_map/all_to_all | solution.py:290

commit v5 on v4

--- a/solution.py
+++ b/solution.py
@@ -78,133 +78,175 @@
     )(part)
 
 
-def filter_kernel(n_plan, n_draw, src_ref, ids_ref, radii_ref, out_ref, field, cx_ref, cy_ref, cz_ref, inv_ref,
-                  send_sem, recv_sem):
+WIDE = 2
+DIRS = ((-1, 0), (1, 0), (0, -1), (0, 1), (-1, -1), (-1, 1), (1, -1), (1, 1))
+
+
+def opposite(k):
+    dp, dd = DIRS[k]
+    return DIRS.index((-dp, -dd))
+
+
+def filter_kernel(n_plan, n_draw, src_ref, ids_ref, radii_ref, out_ref, field, src_e, ids_e, cx_e, cy_e, cz_e,
+                  inv_e, init_send, init_recv, send_sem, recv_sem, credit):
     planes, depth, width = src_ref.shape
+    ext_planes = planes + 2 * WIDE
+    rows = depth + 2 * HALO
+    p = lax.axis_index("plan")
+    d = lax.axis_index("draw")
+
+    def exists(k):
+        dp, dd = DIRS[k]
+        ok_p = (p + dp >= 0) & (p + dp < n_plan)
+        ok_d = (d + dd >= 0) & (d + dd < n_draw)
+        if dp and dd:
+            return ok_p & ok_d
+        return ok_p if dp else ok_d
+
+    def regions(k):
+        dp, dd = DIRS[k]
+        if dp < 0:
+            src_p, dst_p = pl.ds(WIDE, WIDE), pl.ds(WIDE + planes, WIDE)
+        elif dp > 0:
+            src_p, dst_p = pl.ds(planes, WIDE), pl.ds(0, WIDE)
+        else:
+            src_p, dst_p = pl.ds(WIDE, planes), pl.ds(WIDE, planes)
+        if dd < 0:
+            src_r, dst_r = pl.ds(HALO, HALO), pl.ds(HALO + depth, HALO)
+        elif dd > 0:
+            src_r, dst_r = pl.ds(depth, HALO), pl.ds(0, HALO)
+        else:
+            src_r, dst_r = pl.ds(HALO, depth), pl.ds(HALO, depth)
+        return src_p, src_r, dst_p, dst_r
+
+    def target(k):
+        dp, dd = DIRS[k]
+        return (p + dp, d + dd)
+
+    field[...] = jnp.zeros_like(field)
+    src_e[...] = jnp.zeros_like(src_e)
+    ids_e[...] = jnp.zeros_like(ids_e)
     for i in range(planes):
-        cls = ids_ref[i]
-        cx = jnp.zeros((depth, width), jnp.float32)
-        cy = jnp.zeros((depth, width), jnp.float32)
-        cz = jnp.zeros((depth, width), jnp.float32)
+        src_e[WIDE + i, pl.ds(HALO, depth), :] = src_ref[i]
+        ids_e[WIDE + i, pl.ds(HALO, depth), :] = ids_ref[i]
+
+    barrier = pltpu.get_barrier_semaphore()
+    for k in range(len(DIRS)):
+        @pl.when(exists(k))
+        def _():
+            pl.semaphore_signal(barrier, 1, device_id=target(k), device_id_type=MESH)
+    peers = sum(exists(k).astype(jnp.int32) for k in range(len(DIRS)))
+    pl.semaphore_wait(barrier, peers)
+
+    def run(copies):
+        for copy, k in copies:
+            @pl.when(exists(k))
+            def _():
+                copy.start()
+        for copy, k in copies:
+            @pl.when(exists(k))
+            def _():
+                copy.wait_send()
+
+            @pl.when(exists(opposite(k)))
+            def _():
+                copy.wait_recv()
+
+    init = []
+    for which, buf in enumerate((src_e, ids_e)):
+        for k in range(len(DIRS)):
+            sp, sr, dp_, dr = regions(k)
+            init.append((pltpu.make_async_remote_copy(
+                buf.at[sp, sr, :], buf.at[dp_, dr, :], init_send.at[which, k], init_recv.at[which, k],
+                device_id=target(k), device_id_type=MESH), k))
+    run(init)
+
+    row_id = lax.broadcasted_iota(jnp.int32, (rows, width), 0)
+    for i in range(ext_planes):
+        cls = ids_e[i]
+        cx = jnp.zeros((rows, width), jnp.float32)
+        cy = jnp.zeros((rows, width), jnp.float32)
+        cz = jnp.zeros((rows, width), jnp.float32)
         for level in range(radii_ref.shape[0]):
             hit = cls == level
             cx = jnp.where(hit, radii_ref[level, 0], cx)
             cy = jnp.where(hit, radii_ref[level, 1], cy)
             cz = jnp.where(hit, radii_ref[level, 2], cz)
-        cx_ref[i] = cx
-        cy_ref[i] = cy
-        cz_ref[i] = cz
-        inv_ref[i] = 1.0 / (1.0 + 2.0 * (cx + cy + cz))
-    p = lax.axis_index("plan")
-    d = lax.axis_index("draw")
-    has_l = p > 0
-    has_r = p < n_plan - 1
-    has_b = d > 0
-    has_a = d < n_draw - 1
-    lo = HALO
-    hi = HALO + depth
-
-    field[...] = jnp.zeros_like(field)
-    for i in range(planes):
-        field[0, i + 1, pl.ds(lo, depth), :] = src_ref[i]
-
-    barrier = pltpu.get_barrier_semaphore()
-    neighbours = ((has_l, (p - 1, d)), (has_r, (p + 1, d)), (has_b, (p, d - 1)), (has_a, (p, d + 1)))
-    for cond, dev in neighbours:
-        @pl.when(cond)
-        def _():
-            pl.semaphore_signal(barrier, 1, device_id=dev, device_id_type=MESH)
-    peers = sum(cond.astype(jnp.int32) for cond, _ in neighbours)
-    pl.semaphore_wait(barrier, peers)
-
-    def copies(s):
-        to_l = pltpu.make_async_remote_copy(
-            field.at[s, 1, pl.ds(lo, depth), :], field.at[s, planes + 1, pl.ds(lo, depth), :],
-            send_sem.at[s, 0], recv_sem.at[s, 0], device_id=(p - 1, d), device_id_type=MESH)
-        to_r = pltpu.make_async_remote_copy(
-            field.at[s, planes, pl.ds(lo, depth), :], field.at[s, 0, pl.ds(lo, depth), :],
-            send_sem.at[s, 1], recv_sem.at[s, 1], device_id=(p + 1, d), device_id_type=MESH)
-        to_b = pltpu.make_async_remote_copy(
-            field.at[s, pl.ds(1, planes), pl.ds(lo, HALO), :], field.at[s, pl.ds(1, planes), pl.ds(hi, HALO), :],
-            send_sem.at[s, 2], recv_sem.at[s, 2], device_id=(p, d - 1), device_id_type=MESH)
-        to_a = pltpu.make_async_remote_copy(
-            field.at[s, pl.ds(1, planes), pl.ds(hi - HALO, HALO), :], field.at[s, pl.ds(1, planes), pl.ds(0, HALO), :],
-            send_sem.at[s, 3], recv_sem.at[s, 3], device_id=(p, d + 1), device_id_type=MESH)
-        return ((to_l, has_l, has_r), (to_r, has_r, has_l), (to_b, has_b, has_a), (to_a, has_a, has_b))
-
-    def exchange(s):
-        group = copies(s)
-        for copy, send, _ in group:
-            @pl.when(send)
-            def _():
-                copy.start()
-        for copy, send, recv in group:
-            @pl.when(send)
-            def _():
-                copy.wait_send()
-
-            @pl.when(recv)
-            def _():
-                copy.wait_recv()
-
-    lane = lax.broadcasted_iota(jnp.int32, (depth, width), 1)
-
-    def update(s, i, r0, rows, last):
-        at = lo + r0
-        c = field[s, i + 1, pl.ds(at, rows), :]
-        zm = field[s, i + 1, pl.ds(at - 1, rows), :]
-        zp = field[s, i + 1, pl.ds(at + 1, rows), :]
-        xm = field[s, i, pl.ds(at, rows), :]
-        xp = field[s, i + 2, pl.ds(at, rows), :]
-        lanes = lane[:rows]
+        cx_e[i] = cx
+        cy_e[i] = cy
+        cz_e[i] = cz
+        outside = (row_id < HALO) & (d == 0)
+        outside = outside | ((row_id >= HALO + depth) & (d == n_draw - 1))
+        if i < WIDE:
+            outside = outside | (p == 0)
+        if i >= WIDE + planes:
+            outside = outside | (p == n_plan - 1)
+        inv_e[i] = jnp.where(outside, 0.0, 1.0 / (1.0 + 2.0 * (cx + cy + cz)))
+        field[0, i] = src_e[i]
+
+    lane = lax.broadcasted_iota(jnp.int32, (rows, width), 1)
+
+    def wide_update(s, i):
+        c = field[s, i]
+        zm = pltpu.roll(c, 1, 0)
+        zp = pltpu.roll(c, rows - 1, 0)
+        ym = jnp.where(lane == 0, 0.0, pltpu.roll(c, 1, 1))
+        yp = jnp.where(lane == width - 1, 0.0, pltpu.roll(c, width - 1, 1))
+        new = (src_e[i] + cx_e[i] * (field[s, i - 1] + field[s, i + 1]) + cy_e[i] * (ym + yp)
+               + cz_e[i] * (zm + zp)) * inv_e[i]
+        field[1 - s, i] = new
+
+    def core_update(s, i, last):
+        part = pl.ds(HALO, depth)
+        c = field[s, i, part, :]
+        zm = field[s, i, pl.ds(HALO - 1, depth), :]
+        zp = field[s, i, pl.ds(HALO + 1, depth), :]
+        lanes = lane[:depth]
         ym = jnp.where(lanes == 0, 0.0, pltpu.roll(c, 1, 1))
         yp = jnp.where(lanes == width - 1, 0.0, pltpu.roll(c, width - 1, 1))
-        part = pl.ds(r0, rows)
-        new = (src_ref[i, part, :] + cx_ref[i, part, :] * (xm + xp) + cy_ref[i, part, :] * (ym + yp)
-               + cz_ref[i, part, :] * (zm + zp)) * inv_ref[i, part, :]
+        new = (src_e[i, part, :] + cx_e[i, part, :] * (field[s, i - 1, part, :] + field[s, i + 1, part, :])
+               + cy_e[i, part, :] * (ym + yp) + cz_e[i, part, :] * (zm + zp)) * inv_e[i, part, :]
         if last:
-            out_ref[i, part, :] = new
+            out_ref[i - WIDE] = new
         else:
-            field[1 - s, i + 1, pl.ds(at, rows), :] = new
-
-    def sweep_send(s):
-        t = 1 - s
-        group = copies(t)
-        update(s, 0, 0, depth, False)
-        update(s, planes - 1, 0, depth, False)
-        for copy, send, _ in group[:2]:
-            @pl.when(send)
-            def _():
-                copy.start()
-        for i in range(1, planes - 1):
-            update(s, i, 0, HALO, False)
-            update(s, i, depth - HALO, HALO, False)
-        for copy, send, _ in group[2:]:
-            @pl.when(send)
-            def _():
-                copy.start()
-        for i in range(1, planes - 1):
-            update(s, i, HALO, depth - 2 * HALO, False)
-        for copy, send, recv in group:
-            @pl.when(send)
-            def _():
-                copy.wait_send()
-
-            @pl.when(recv)
-            def _():
-                copy.wait_recv()
-
-    exchange(0)
-
-    def pair(k, carry):
-        sweep_send(0)
-        sweep_send(1)
+            field[1 - s, i, part, :] = new
+
+    def group(first, last):
+        if not first:
+            copies = []
+            for k in range(len(DIRS)):
+                sp, sr, dp_, dr = regions(k)
+
+                @pl.when(exists(k))
+                def _():
+                    pl.semaphore_wait(credit.at[opposite(k)], 1)
+                copies.append((pltpu.make_async_remote_copy(
+                    field.at[0, sp, sr, :], field.at[0, dp_, dr, :], send_sem.at[k], recv_sem.at[k],
+                    device_id=target(k), device_id_type=MESH), k))
+            run(copies)
+        for j in range(WIDE):
+            s = j % 2
+            e = WIDE - 1 - j
+            if e > 0:
+                for i in range(WIDE - e, WIDE + planes + e):
+                    wide_update(s, i)
+            else:
+                for i in range(WIDE, WIDE + planes):
+                    core_update(s, i, last)
+            if j == 0 and not last:
+                for k in range(len(DIRS)):
+                    @pl.when(exists(k))
+                    def _():
+                        pl.semaphore_signal(credit.at[k], 1, device_id=target(k), device_id_type=MESH)
+
+    group(True, False)
+
+    def middle(g, carry):
+        group(False, False)
         return carry
 
-    lax.fori_loop(0, SWEEPS // 2 - 1, pair, 0)
-    sweep_send(0)
-    for i in range(planes):
-        update(1, i, 0, depth, True)
+    lax.fori_loop(0, SWEEPS // WIDE - 2, middle, 0)
+    group(False, True)
 
 
 def smooth_each(source, class_ids, class_radii, n_plan, n_draw, kid):
@@ -217,13 +259,18 @@
         in_specs=[vmem, vmem, smem],
         out_specs=vmem,
         scratch_shapes=[
-            pltpu.VMEM((2, planes + 2, depth + 2 * HALO, width), jnp.float32),
-            pltpu.VMEM(source.shape, jnp.float32),
-            pltpu.VMEM(source.shape, jnp.float32),
-            pltpu.VMEM(source.shape, jnp.float32),
-            pltpu.VMEM(source.shape, jnp.float32),
-            pltpu.SemaphoreType.DMA((2, 4)),
-            pltpu.SemaphoreType.DMA((2, 4)),
+            pltpu.VMEM((2, planes + 2 * WIDE, depth + 2 * HALO, width), jnp.float32),
+            pltpu.VMEM((planes + 2 * WIDE, depth + 2 * HALO, width), jnp.float32),
+            pltpu.VMEM((planes + 2 * WIDE, depth + 2 * HALO, width), jnp.int32),
+            pltpu.VMEM((planes + 2 * WIDE, depth + 2 * HALO, width), jnp.float32),
+            pltpu.VMEM((planes + 2 * WIDE, depth + 2 * HALO, width), jnp.float32),
+            pltpu.VMEM((planes + 2 * WIDE, depth + 2 * HALO, width), jnp.float32),
+            pltpu.VMEM((planes + 2 * WIDE, depth + 2 * HALO, width), jnp.float32),
+            pltpu.SemaphoreType.DMA((2, len(DIRS))),
+            pltpu.SemaphoreType.DMA((2, len(DIRS))),
+            pltpu.SemaphoreType.DMA((len(DIRS),)),
+            pltpu.SemaphoreType.DMA((len(DIRS),)),
+            pltpu.SemaphoreType.REGULAR((len(DIRS),)),
         ],
         compiler_params=pltpu.CompilerParams(collective_id=kid, has_side_effects=True),
     )(source, class_ids, class_radii)

time: 245 us -> 247 us (level)
  Pallas kernels: 151 us -> 157 us
  starting transfers between devices: 17.5 us -> 13.4 us
    pallas_call x2, Pallas kernels: 135 us -> 141 us  [smooth_each(): pl.pallas_call(functools.partial(filter_kernel, n_plan, n_draw), out_shap...]
    all_to_all x1, starting transfers between devices: 17.5 us -> 13.4 us  [per_device(): lax.all_to_all(sendbuf, 'plan', split_axis=0, concat_axis=0, tiled=True)]
where the time goes in v5:
time: 247 us
  Pallas kernels  157 us (64%)
  local copies, waits for them, and re-layouts  29.1 us (12%)
  waiting for transfers between devices  28.4 us (11%)
  starting transfers between devices  13.4 us (5%)
  other arithmetic  13 us (5%)
  matrix products  5.32 us (2%)
    pallas_call x2, Pallas kernels, smooth_each(): pl.pallas_call(functools.partial(filter_kernel, n_plan, n_draw), out_shap...  141 us
    all_to_all x1, waiting for transfers between devices, per_device(): lax.all_to_all(sendbuf, 'plan', split_axis=0, concat_axis=0, tiled=True)  28.4 us
    gather x1, local copies, waits for them, and re-layouts, per_device(): packed = jnp.take(table, source_row, axis=0)  16.1 us
    pallas_call x2, Pallas kernels, entering(): pl.pallas_call(functools.partial(scan_kernel, n_draw, reverse), out_shape...  15.5 us
    all_to_all x1, starting transfers between devices, per_device(): lax.all_to_all(sendbuf, 'plan', split_axis=0, concat_axis=0, tiled=True)  13.4 us
    unnamed x20, local copies, waits for them, and re-layouts  6.24 us
  transfers between devices with their start and end apart: 1, of which 1 were waited for; matrix products, arithmetic and copies ran while one was open for 1% of the time, Pallas kernels for 0%

profile of v5, /device:TPU:1, one launch (start us, length us, event | category | flops | bytes accessed | tf_op | source)
XLA Modules:
  0.0 246.6 jit_solution(10473195343890753732)
XLA Ops:
  0.6 0.0 copy-start.2
  0.6 0.0 copy-start.5
  0.7 0.8 add_select_fusion
  1.4 0.5 fusion.5
  2.0 0.7 compare_select_fusion.1
  2.7 4.3 %scatter_custom_fusion = s32[4096]{0:T(1024)S(1)} fusion(s32[1024]{0:T(1024)S(1)} %bitcast.44, s32[1024]{0:T(1024)S(1)} %iota.17, s32[]{:T(128)} %constant.68.clone.1), kind=kCustom, calls=%fused_computation.43 | custom fusion | bytes 16388 | tf_op jit(solution)/shard_map/scatter | solution.py:322
  7.1 2.0 copy.18
  9.1 0.0 copy-done.2
  9.1 0.0 copy-start.3
  9.1 1.0 copy.19
  10.1 0.0 copy-done.5
  10.1 0.7 copy.20.radii_ref
  10.8 69.1 %shard_map.76 = f32[8,128,128]{2,1,0:T(8,128)} custom-call(f32[8,128,128]{2,1,0:T(8,128)} %bitcast.37, s32[8,128,128]{2,1,0:T(8,128)} %bitcast.34, f32[8,3]{1,0:T(8,128)} %copy.20.radii_ref), custom_call_target="tpu_custom_call" | custom-call | tf_op jit(solution)/shard_map/pallas_call | solution.py:256
  79.9 0.0 copy-start
  79.9 1.3 fusion.14
  81.1 0.3 fusion.11
  81.5 0.6 slice_bitcast_fusion.1.part_ref
  82.1 6.9 %shard_map.77 = f32[8,128]{1,0:T(8,128)} custom-call(f32[8,128]{1,0:T(8,128)} %slice_bitcast_fusion.1.part_ref), custom_call_target="tpu_custom_call" | custom-call | tf_op jit(solution)/shard_map/pallas_call | solution.py:67
  89.0 0.0 copy-done.3
  89.0 0.2 copy.22
  89.2 2.1 fusion.6
  91.3 0.6 slice_bitcast_fusion.part_ref
  91.9 8.6 %shard_map.78 = f32[8,128]{1,0:T(8,128)} custom-call(f32[8,128]{1,0:T(8,128)} %slice_bitcast_fusion.part_ref), custom_call_target="tpu_custom_call" | custom-call | tf_op jit(solution)/shard_map/pallas_call | solution.py:67
  100.5 0.0 copy-done
  100.5 0.0 copy-start.6
  100.5 1.8 fusion.10.src_ref
  102.3 72.0 %shard_map.79 = f32[8,128,128]{2,1,0:T(8,128)} custom-call(f32[8,128,128]{2,1,0:T(8,128)} %fusion.10.src_ref, s32[8,128,128]{2,1,0:T(8,128)} %bitcast.35, f32[8,3]{1,0:T(8,128)} %copy.20.radii_ref), custom_call_target="tpu_custom_call" | custom-call | tf_op jit(solution)/shard_map/pallas_call | solution.py:256
  174.3 1.2 copy.28
  175.6 0.0 copy-start.1
  175.6 0.2 broadcast_in_dim.34
  175.8 0.0 copy-done.6
  175.8 0.1 pad_maximum_fusion
  175.9 16.1 %gather_fusion = f32[4096,256]{1,0:T(8,128)} fusion(f32[1025,256]{1,0:T(8,128)S(1)} %pad_maximum_fusion, s32[4096]{0:T(1024)S(1)} %fusion.20), kind=kCustom, calls=%fused_computation | custom fusion | bytes 8404992 | tf_op jit(solution)/shard_map/jit(_take)/gather | solution.py:327
  191.9 0.0 copy-done.1
  191.9 4.1 %broadcast_select_fusion = f32[4096,256]{1,0:T(8,128)S(1)} fusion(f32[4096,256]{1,0:T(8,128)} %gather_fusion, pred[4096]{0:T(1024)(128)(4,1)S(1)} %compare_and_fusion), kind=kLoop, calls=%fused_computation.9 | loop fusion | flops 1048576 | bytes 8392704 | tf_op jit(solution)/shard_map/jit(_take)/select_n | solution.py:327
  196.0 0.6 slice_reduce_fusion
  196.7 0.1 slice.28
  196.8 0.1 pad.2.clone
  196.9 1.6 maximum_maximum_fusion
  198.5 0.0 copy-start.4
  198.5 13.4 %all-to-all-start = ((f32[32,136,128]{2,1,0:T(8,128)}), f32[32,136,128]{2,1,0:T(8,128)S(1)}, u32[]{:S(2)}, u32[]{:S(2)}) async-start(f32[32,136,128]{2,1,0:T(8,128)} %maximum_maximum_fusion), calls=%async_computation | async-start | bytes 4456448 | tf_op jit(solution)/shard_map/all_to_all | solution.py:337
  211.9 0.0 copy-done.4
  211.9 0.3 power_bitcast_fusion
  212.2 1.0 copy.27
  213.2 28.4 %all-to-all-done = f32[32,136,128]{2,1,0:T(8,128)S(1)} async-done(((f32[32,136,128]{2,1,0:T(8,128)}), f32[32,136,128]{2,1,0:T(8,128)S(1)}, u32[]{:S(2)}, u32[]{:S(2)}) %all-to-all-start) | async-done | bytes 2228256 | tf_op jit(solution)/shard_map/all_to_all | solution.py:337
  241.6 0.2 slice.31
  241.9 4.8 %fusion.3 = f32[512,128]{1,0:T(8,128)} fusion(f32[4096,128]{1,0:T(8,128)S(1)} %bitcast.38, s32[4096]{0:T(1024)S(1)} %bitcast.43), kind=kOutput, calls=%fused_computation.10 | convolution fusion | flops 3223388160 | bytes 2375680 | tf_op jit(solution)/shard_map/dot_general | solution.py:343
  (6 shorter events, 0.0 us)
Async XLA Ops:
  0.6 8.5 %copy-start.2 = (s32[8,128,128]{2,1,0:T(8,128)S(1)}, s32[8,128,128]{2,1,0:T(8,128)}, u32[]{:S(2)}) copy-start(s32[8,128,128]{2,1,0:T(8,128)} %param.6) | copy-start | bytes 1572868
  0.6 9.5 %copy-start.5 = (f32[8,3]{0,1:T(4,128)S(1)}, f32[8,3]{0,1:T(4,128)}, u32[]{:S(2)}) copy-start(f32[8,3]{0,1:T(4,128)} %param.7) | copy-start | bytes 292
  9.1 79.9 %copy-start.3 = (f32[8,128,128]{2,1,0:T(8,128)S(1)}, f32[8,128,128]{2,1,0:T(8,128)}, u32[]{:S(2)}) copy-start(f32[8,128,128]{2,1,0:T(8,128)} %param.8) | copy-start | bytes 1572868
  79.9 20.6 %copy-start = (f32[8,128,128]{2,1,0:T(8,128)S(1)}, f32[8,128,128]{2,1,0:T(8,128)}, u32[]{:S(2)}) copy-start(f32[8,128,128]{2,1,0:T(8,128)} %shard_map.76) | copy-start | bytes 1572868
  100.5 75.3 %copy-start.6 = (f32[1,256]{1,0:T(1,128)S(1)}, f32[1,256]{1,0:T(1,128)}, u32[]{:S(2)}) copy-start(f32[1,256]{1,0:T(1,128)} %constant.78.clone.1) | copy-start | bytes 3076
  175.6 16.4 %copy-start.1 = (f32[8,128,128]{2,1,0:T(8,128)}, f32[8,128,128]{2,1,0:T(8,128)S(1)}, u32[]{:S(2)}) copy-start(f32[8,128,128]{2,1,0:T(8,128)S(1)} %copy.28) | copy-start | bytes 1572868
  198.5 13.4 %copy-start.4 = (f32[8,128]{1,0:T(8,128)S(1)}, f32[8,128]{1,0:T(8,128)}, u32[]{:S(2)}) copy-start(f32[8,128]{1,0:T(8,128)} %shard_map.77) | copy-start | bytes 12292
  198.5 43.1 %all-to-all-start = ((f32[32,136,128]{2,1,0:T(8,128)}), f32[32,136,128]{2,1,0:T(8,128)S(1)}, u32[]{:S(2)}, u32[]{:S(2)}) async-start(f32[32,136,128]{2,1,0:T(8,128)} %maximum_maximum_fusion), calls=%async_computation | async-start | bytes 4456448 | tf_op jit(solution)/shard_map/all_to_all | solution.py:337

commit v6 on v4

--- a/solution.py
+++ b/solution.py
@@ -205,6 +205,53 @@
     sweep_send(0)
     for i in range(planes):
         update(1, i, 0, depth, True)
+
+
+def exchange_kernel(n_plan, send_ref, out_ref, send_sem, recv_sem, local_sem):
+    p = lax.axis_index("plan")
+    d = lax.axis_index("draw")
+    barrier = pltpu.get_barrier_semaphore()
+    for e in range(n_plan):
+        @pl.when(e != p)
+        def _():
+            pl.semaphore_signal(barrier, 1, device_id=(e, d), device_id_type=MESH)
+    pl.semaphore_wait(barrier, n_plan - 1)
+    local = pltpu.make_async_copy(send_ref.at[p], out_ref.at[p], local_sem)
+    local.start()
+    sends = []
+    for e in range(n_plan):
+        copy = pltpu.make_async_remote_copy(
+            send_ref.at[e], out_ref.at[p], send_sem.at[e], recv_sem.at[p], device_id=(e, d), device_id_type=MESH)
+        sends.append(copy)
+
+        @pl.when(e != p)
+        def _():
+            copy.start()
+    for e in range(n_plan):
+        incoming = pltpu.make_async_remote_copy(
+            send_ref.at[e], out_ref.at[e], send_sem.at[e], recv_sem.at[e], device_id=(e, d), device_id_type=MESH)
+
+        @pl.when(e != p)
+        def _():
+            sends[e].wait_send()
+            incoming.wait_recv()
+    local.wait()
+
+
+def exchange_rows(sendbuf, n_plan, kid):
+    vmem = pl.BlockSpec(memory_space=pltpu.VMEM)
+    return pl.pallas_call(
+        functools.partial(exchange_kernel, n_plan),
+        out_shape=jax.ShapeDtypeStruct(sendbuf.shape, jnp.float32),
+        in_specs=[vmem],
+        out_specs=vmem,
+        scratch_shapes=[
+            pltpu.SemaphoreType.DMA((n_plan,)),
+            pltpu.SemaphoreType.DMA((n_plan,)),
+            pltpu.SemaphoreType.DMA(()),
+        ],
+        compiler_params=pltpu.CompilerParams(collective_id=kid, has_side_effects=True),
+    )(sendbuf)
 
 
 def smooth_each(source, class_ids, class_radii, n_plan, n_draw, kid):
@@ -287,7 +334,7 @@
         ],
         axis=1,
     )
-    arrived_all = lax.all_to_all(sendbuf, "plan", split_axis=0, concat_axis=0, tiled=True)
+    arrived_all = exchange_rows(sendbuf, n_plan, 4)
     arrived = arrived_all[:, :capacity, :]
     arrived_ids = arrived_all[:, capacity:capacity + id_rows, :]
     picks = (

time: 245 us -> 265 us (1.082)
  the two profiles are of different devices: /device:TPU:1 before, /device:TPU:29 now
where the time goes in v6:
time: 265 us
  Pallas kernels  214 us (81%)
  local copies, waits for them, and re-layouts  32.5 us (12%)
  other arithmetic  12.5 us (5%)
  matrix products  5.31 us (2%)
    pallas_call x2, Pallas kernels, smooth_each(): pl.pallas_call(functools.partial(filter_kernel, n_plan, n_draw), out_shap...  142 us
    pallas_call x1, Pallas kernels, exchange_rows(): pl.pallas_call(functools.partial(exchange_kernel, n_plan), out_shape=jax....  53.4 us
    pallas_call x2, Pallas kernels, entering(): pl.pallas_call(functools.partial(scan_kernel, n_draw, reverse), out_shape...  17.7 us
    gather x1, local copies, waits for them, and re-layouts, per_device(): packed = jnp.take(table, source_row, axis=0)  16.1 us
    unnamed x18, local copies, waits for them, and re-layouts  7.95 us

profile of v6, /device:TPU:29, one launch (start us, length us, event | category | flops | bytes accessed | tf_op | source)
XLA Modules:
  0.0 264.7 jit_solution(14073825490063101579)
XLA Ops:
  0.6 2.0 copy.17
  2.7 2.0 copy.18
  4.7 1.3 copy.19.radii_ref
  6.0 70.1 %shard_map.76 = f32[8,128,128]{2,1,0:T(8,128)} custom-call(f32[8,128,128]{2,1,0:T(8,128)} %bitcast.37, s32[8,128,128]{2,1,0:T(8,128)} %bitcast.34, f32[8,3]{1,0:T(8,128)} %copy.19.radii_ref), custom_call_target="tpu_custom_call" | custom-call | tf_op jit(solution)/shard_map/pallas_call | solution.py:261
  76.1 0.0 copy-start.2
  76.1 1.3 fusion.14
  77.4 0.3 fusion.11
  77.7 0.6 slice_bitcast_fusion.1.part_ref
  78.3 7.9 %shard_map.77 = f32[8,128]{1,0:T(8,128)} custom-call(f32[8,128]{1,0:T(8,128)} %slice_bitcast_fusion.1.part_ref), custom_call_target="tpu_custom_call" | custom-call | tf_op jit(solution)/shard_map/pallas_call | solution.py:67
  86.2 0.0 copy-start.3
  86.2 0.0 copy-start
  86.2 1.0 power_bitcast_fusion
  87.2 1.0 copy.26
  88.3 0.0 copy-done.2
  88.3 0.2 copy.21
  88.5 0.0 copy-done.3
  88.5 1.4 fusion.6
  89.9 0.0 copy-start.4
  89.9 0.6 slice_bitcast_fusion.part_ref
  90.5 9.8 %shard_map.78 = f32[8,128]{1,0:T(8,128)} custom-call(f32[8,128]{1,0:T(8,128)} %slice_bitcast_fusion.part_ref), custom_call_target="tpu_custom_call" | custom-call | tf_op jit(solution)/shard_map/pallas_call | solution.py:67
  100.3 0.0 copy-done
  100.3 0.0 copy-start.5
  100.3 1.8 fusion.10.src_ref
  102.1 72.3 %shard_map.79 = f32[8,128,128]{2,1,0:T(8,128)} custom-call(f32[8,128,128]{2,1,0:T(8,128)} %fusion.10.src_ref, s32[8,128,128]{2,1,0:T(8,128)} %bitcast.35, f32[8,3]{1,0:T(8,128)} %copy.19.radii_ref), custom_call_target="tpu_custom_call" | custom-call | tf_op jit(solution)/shard_map/pallas_call | solution.py:261
  174.5 1.2 copy.27
  175.7 0.0 copy-start.1
  175.7 0.0 copy-done.4
  175.7 0.2 broadcast_in_dim.34
  175.9 0.0 copy-done.5
  176.0 0.1 pad_maximum_fusion
  176.0 0.5 fusion.5
  176.6 4.5 %scatter_custom_fusion = s32[4096]{0:T(1024)S(1)} fusion(s32[1024]{0:T(1024)S(1)} %bitcast.44, s32[1024]{0:T(1024)S(1)} %iota.17, s32[]{:T(128)} %constant.68.clone.1), kind=kCustom, calls=%fused_computation.43 | custom fusion | bytes 16388 | tf_op jit(solution)/shard_map/scatter | solution.py:322
  181.2 16.1 %gather_fusion = f32[4096,256]{1,0:T(8,128)} fusion(f32[1025,256]{1,0:T(8,128)S(1)} %pad_maximum_fusion, s32[4096]{0:T(1024)S(1)} %fusion.20), kind=kCustom, calls=%fused_computation | custom fusion | bytes 8404992 | tf_op jit(solution)/shard_map/jit(_take)/gather | solution.py:327
  197.2 0.0 copy-done.1
  197.3 4.1 %broadcast_select_fusion = f32[4096,256]{1,0:T(8,128)S(1)} fusion(f32[4096,256]{1,0:T(8,128)} %gather_fusion, pred[4096]{0:T(1024)(128)(4,1)S(1)} %compare_and_fusion), kind=kLoop, calls=%fused_computation.9 | loop fusion | flops 1048576 | bytes 8392704 | tf_op jit(solution)/shard_map/jit(_take)/select_n | solution.py:327
  201.4 0.6 slice_reduce_fusion
  202.0 0.1 slice.28
  202.1 0.1 pad.2.clone
  202.2 1.6 maximum_maximum_fusion.send_ref
  203.8 53.4 %shard_map.80 = f32[32,136,128]{2,1,0:T(8,128)} custom-call(f32[32,136,128]{2,1,0:T(8,128)} %maximum_maximum_fusion.send_ref), custom_call_target="tpu_custom_call" | custom-call | tf_op jit(solution)/shard_map/pallas_call | solution.py:243
  257.3 1.7 slice.23
  259.0 0.9 slice_convert_fusion
  259.9 4.8 %fusion.3 = f32[512,128]{1,0:T(8,128)} fusion(f32[4096,128]{1,0:T(8,128)S(1)} %bitcast.38, s32[4096]{0:T(1024)S(1)} %bitcast.43), kind=kOutput, calls=%fused_computation.10 | convolution fusion | flops 3223388160 | bytes 2375680 | tf_op jit(solution)/shard_map/dot_general | solution.py:343
  (7 shorter events, 0.1 us)
Async XLA Ops:
  76.1 12.1 %copy-start.2 = (f32[8,128,128]{2,1,0:T(8,128)S(1)}, f32[8,128,128]{2,1,0:T(8,128)}, u32[]{:S(2)}) copy-start(f32[8,128,128]{2,1,0:T(8,128)} %param.8) | copy-start | bytes 1572868
  86.2 2.3 copy-start.3
  86.2 14.1 %copy-start = (f32[8,128,128]{2,1,0:T(8,128)S(1)}, f32[8,128,128]{2,1,0:T(8,128)}, u32[]{:S(2)}) copy-start(f32[8,128,128]{2,1,0:T(8,128)} %shard_map.76) | copy-start | bytes 1572868
  89.9 85.8 %copy-start.4 = (s32[1,1,1024]{2,1,0:T(1,128)S(1)}, s32[1,1,1024]{2,1,0:T(1,128)}, u32[]{:S(2)}) copy-start(s32[1,1,1024]{2,1,0:T(1,128)} %param.9) | copy-start | bytes 12292
  100.3 75.6 %copy-start.5 = (f32[1,256]{1,0:T(1,128)S(1)}, f32[1,256]{1,0:T(1,128)}, u32[]{:S(2)}) copy-start(f32[1,256]{1,0:T(1,128)} %constant.78.clone.1) | copy-start | bytes 3076
  175.7 21.5 %copy-start.1 = (f32[8,128,128]{2,1,0:T(8,128)}, f32[8,128,128]{2,1,0:T(8,128)S(1)}, u32[]{:S(2)}) copy-start(f32[8,128,128]{2,1,0:T(8,128)S(1)} %copy.27) | copy-start | bytes 1572868

commit v7 on v4

--- a/solution.py
+++ b/solution.py
@@ -139,13 +139,15 @@
             def _():
                 copy.start()
         for copy, send, recv in group:
+            @pl.when(recv)
+            def _():
+                copy.wait_recv()
+
+    def sent(s):
+        for copy, send, _ in copies(s):
             @pl.when(send)
             def _():
                 copy.wait_send()
-
-            @pl.when(recv)
-            def _():
-                copy.wait_recv()
 
     lane = lax.broadcasted_iota(jnp.int32, (depth, width), 1)
 
@@ -186,13 +188,10 @@
         for i in range(1, planes - 1):
             update(s, i, HALO, depth - 2 * HALO, False)
         for copy, send, recv in group:
-            @pl.when(send)
-            def _():
-                copy.wait_send()
-
             @pl.when(recv)
             def _():
                 copy.wait_recv()
+        sent(s)
 
     exchange(0)
 
@@ -205,6 +204,7 @@
     sweep_send(0)
     for i in range(planes):
         update(1, i, 0, depth, True)
+    sent(1)
 
 
 def smooth_each(source, class_ids, class_radii, n_plan, n_draw, kid):

time: 245 us -> 245 us (level)
  no operation moved by 1% of the time
where the time goes in v7:
time: 245 us
  Pallas kernels  151 us (62%)
  local copies, waits for them, and re-layouts  29.1 us (12%)
  waiting for transfers between devices  28.4 us (12%)
  starting transfers between devices  17.5 us (7%)
  other arithmetic  13 us (5%)
  matrix products  5.32 us (2%)
    pallas_call x2, Pallas kernels, smooth_each(): pl.pallas_call(functools.partial(filter_kernel, n_plan, n_draw), out_shap...  135 us
    all_to_all x1, waiting for transfers between devices, per_device(): lax.all_to_all(sendbuf, 'plan', split_axis=0, concat_axis=0, tiled=True)  28.4 us
    all_to_all x1, starting transfers between devices, per_device(): lax.all_to_all(sendbuf, 'plan', split_axis=0, concat_axis=0, tiled=True)  17.5 us
    gather x1, local copies, waits for them, and re-layouts, per_device(): packed = jnp.take(table, source_row, axis=0)  16.1 us
    pallas_call x2, Pallas kernels, entering(): pl.pallas_call(functools.partial(scan_kernel, n_draw, reverse), out_shape...  15.9 us
    unnamed x20, local copies, waits for them, and re-layouts  6.24 us
  transfers between devices with their start and end apart: 1, of which 1 were waited for; matrix products, arithmetic and copies ran while one was open for 1% of the time, Pallas kernels for 0%

profile of v7, /device:TPU:1, one launch (start us, length us, event | category | flops | bytes accessed | tf_op | source)
XLA Modules:
  0.0 244.8 jit_solution(14584691172772810787)
XLA Ops:
  0.6 0.0 copy-start.2
  0.6 0.0 copy-start.5
  0.7 0.8 add_select_fusion
  1.4 0.5 fusion.5
  2.0 0.7 compare_select_fusion.1
  2.7 4.3 %scatter_custom_fusion = s32[4096]{0:T(1024)S(1)} fusion(s32[1024]{0:T(1024)S(1)} %bitcast.44, s32[1024]{0:T(1024)S(1)} %iota.17, s32[]{:T(128)} %constant.68.clone.1), kind=kCustom, calls=%fused_computation.43 | custom fusion | bytes 16388 | tf_op jit(solution)/shard_map/scatter | solution.py:275
  7.1 2.0 copy.18
  9.1 0.0 copy-done.2
  9.1 0.0 copy-start.3
  9.1 1.0 copy.19
  10.1 0.0 copy-done.5
  10.1 0.7 copy.20.radii_ref
  10.8 68.4 %shard_map.76 = f32[8,128,128]{2,1,0:T(8,128)} custom-call(f32[8,128,128]{2,1,0:T(8,128)} %bitcast.37, s32[8,128,128]{2,1,0:T(8,128)} %bitcast.34, f32[8,3]{1,0:T(8,128)} %copy.20.radii_ref), custom_call_target="tpu_custom_call" | custom-call | tf_op jit(solution)/shard_map/pallas_call | solution.py:214
  79.2 0.0 copy-start
  79.2 1.3 fusion.14
  80.5 0.3 fusion.11
  80.8 0.6 slice_bitcast_fusion.1.part_ref
  81.4 6.8 %shard_map.77 = f32[8,128]{1,0:T(8,128)} custom-call(f32[8,128]{1,0:T(8,128)} %slice_bitcast_fusion.1.part_ref), custom_call_target="tpu_custom_call" | custom-call | tf_op jit(solution)/shard_map/pallas_call | solution.py:67
  88.3 0.0 copy-done.3
  88.3 0.2 copy.22
  88.5 2.1 fusion.6
  90.6 0.6 slice_bitcast_fusion.part_ref
  91.2 9.0 %shard_map.78 = f32[8,128]{1,0:T(8,128)} custom-call(f32[8,128]{1,0:T(8,128)} %slice_bitcast_fusion.part_ref), custom_call_target="tpu_custom_call" | custom-call | tf_op jit(solution)/shard_map/pallas_call | solution.py:67
  100.2 0.0 copy-done
  100.2 0.0 copy-start.6
  100.2 1.8 fusion.10.src_ref
  102.0 66.3 %shard_map.79 = f32[8,128,128]{2,1,0:T(8,128)} custom-call(f32[8,128,128]{2,1,0:T(8,128)} %fusion.10.src_ref, s32[8,128,128]{2,1,0:T(8,128)} %bitcast.35, f32[8,3]{1,0:T(8,128)} %copy.20.radii_ref), custom_call_target="tpu_custom_call" | custom-call | tf_op jit(solution)/shard_map/pallas_call | solution.py:214
  168.3 1.2 copy.28
  169.5 0.0 copy-start.1
  169.6 0.2 broadcast_in_dim.34
  169.8 0.0 copy-done.6
  169.8 0.1 pad_maximum_fusion
  169.8 16.1 %gather_fusion = f32[4096,256]{1,0:T(8,128)} fusion(f32[1025,256]{1,0:T(8,128)S(1)} %pad_maximum_fusion, s32[4096]{0:T(1024)S(1)} %fusion.20), kind=kCustom, calls=%fused_computation | custom fusion | bytes 8404992 | tf_op jit(solution)/shard_map/jit(_take)/gather | solution.py:280
  185.9 0.0 copy-done.1
  185.9 4.1 %broadcast_select_fusion = f32[4096,256]{1,0:T(8,128)S(1)} fusion(f32[4096,256]{1,0:T(8,128)} %gather_fusion, pred[4096]{0:T(1024)(128)(4,1)S(1)} %compare_and_fusion), kind=kLoop, calls=%fused_computation.9 | loop fusion | flops 1048576 | bytes 8392704 | tf_op jit(solution)/shard_map/jit(_take)/select_n | solution.py:280
  190.0 0.6 slice_reduce_fusion
  190.6 0.1 slice.28
  190.8 0.1 pad.2.clone
  190.9 1.6 maximum_maximum_fusion
  192.5 0.0 copy-start.4
  192.5 17.5 %all-to-all-start = ((f32[32,136,128]{2,1,0:T(8,128)}), f32[32,136,128]{2,1,0:T(8,128)S(1)}, u32[]{:S(2)}, u32[]{:S(2)}) async-start(f32[32,136,128]{2,1,0:T(8,128)} %maximum_maximum_fusion), calls=%async_computation | async-start | bytes 4456448 | tf_op jit(solution)/shard_map/all_to_all | solution.py:290
  210.0 0.0 copy-done.4
  210.0 0.3 power_bitcast_fusion
  210.3 1.0 copy.27
  211.4 28.4 %all-to-all-done = f32[32,136,128]{2,1,0:T(8,128)S(1)} async-done(((f32[32,136,128]{2,1,0:T(8,128)}), f32[32,136,128]{2,1,0:T(8,128)S(1)}, u32[]{:S(2)}, u32[]{:S(2)}) %all-to-all-start) | async-done | bytes 2228256 | tf_op jit(solution)/shard_map/all_to_all | solution.py:290
  239.7 0.2 slice.31
  240.0 4.8 %fusion.3 = f32[512,128]{1,0:T(8,128)} fusion(f32[4096,128]{1,0:T(8,128)S(1)} %bitcast.38, s32[4096]{0:T(1024)S(1)} %bitcast.43), kind=kOutput, calls=%fused_computation.10 | convolution fusion | flops 3223388160 | bytes 2375680 | tf_op jit(solution)/shard_map/dot_general | solution.py:296
  (6 shorter events, 0.0 us)
Async XLA Ops:
  0.6 8.5 %copy-start.2 = (s32[8,128,128]{2,1,0:T(8,128)S(1)}, s32[8,128,128]{2,1,0:T(8,128)}, u32[]{:S(2)}) copy-start(s32[8,128,128]{2,1,0:T(8,128)} %param.6) | copy-start | bytes 1572868
  0.6 9.5 %copy-start.5 = (f32[8,3]{0,1:T(4,128)S(1)}, f32[8,3]{0,1:T(4,128)}, u32[]{:S(2)}) copy-start(f32[8,3]{0,1:T(4,128)} %param.7) | copy-start | bytes 292
  9.1 79.2 %copy-start.3 = (f32[8,128,128]{2,1,0:T(8,128)S(1)}, f32[8,128,128]{2,1,0:T(8,128)}, u32[]{:S(2)}) copy-start(f32[8,128,128]{2,1,0:T(8,128)} %param.8) | copy-start | bytes 1572868
  79.2 21.0 %copy-start = (f32[8,128,128]{2,1,0:T(8,128)S(1)}, f32[8,128,128]{2,1,0:T(8,128)}, u32[]{:S(2)}) copy-start(f32[8,128,128]{2,1,0:T(8,128)} %shard_map.76) | copy-start | bytes 1572868
  100.2 69.6 %copy-start.6 = (f32[1,256]{1,0:T(1,128)S(1)}, f32[1,256]{1,0:T(1,128)}, u32[]{:S(2)}) copy-start(f32[1,256]{1,0:T(1,128)} %constant.78.clone.1) | copy-start | bytes 3076
  169.5 16.4 %copy-start.1 = (f32[8,128,128]{2,1,0:T(8,128)}, f32[8,128,128]{2,1,0:T(8,128)S(1)}, u32[]{:S(2)}) copy-start(f32[8,128,128]{2,1,0:T(8,128)S(1)} %copy.28) | copy-start | bytes 1572868
  192.5 17.6 %copy-start.4 = (f32[8,128]{1,0:T(8,128)S(1)}, f32[8,128]{1,0:T(8,128)}, u32[]{:S(2)}) copy-start(f32[8,128]{1,0:T(8,128)} %shard_map.77) | copy-start | bytes 12292
  192.5 47.3 %all-to-all-start = ((f32[32,136,128]{2,1,0:T(8,128)}), f32[32,136,128]{2,1,0:T(8,128)S(1)}, u32[]{:S(2)}, u32[]{:S(2)}) async-start(f32[32,136,128]{2,1,0:T(8,128)} %maximum_maximum_fusion), calls=%async_computation | async-start | bytes 4456448 | tf_op jit(solution)/shard_map/all_to_all | solution.py:290

commit v8 on v4

--- a/solution.py
+++ b/solution.py
@@ -272,21 +272,17 @@
     counted = jnp.dot(upto, onehot, preferred_element_type=jnp.float32)
     ranking = jnp.sum(counted * onehot.astype(jnp.float32), axis=1).astype(jnp.int32) - 1
     position = owners * capacity + ranking
-    source_row = jnp.full((tiles * capacity,), row_count, jnp.int32).at[position].set(rows)
-    table = jnp.concatenate(
-        [row_data, jnp.broadcast_to(slot_patch.astype(jnp.float32)[:, None], (row_count, depth))], axis=1)
-    table = jnp.concatenate(
-        [table, jnp.concatenate([jnp.zeros((1, depth), jnp.float32), jnp.full((1, depth), float(PATCH_DEV))], axis=1)])
-    packed = jnp.take(table, source_row, axis=0)
+    slots = tiles * capacity
+    source_row = jnp.full((slots,), row_count, jnp.int32).at[position].set(rows)
+    send_ids = jnp.full((slots,), float(PATCH_DEV), jnp.float32).at[position].set(slot_patch.astype(jnp.float32))
     id_rows = capacity // depth
-    sendbuf = jnp.concatenate(
-        [
-            packed[:, :depth].reshape(tiles, capacity, depth),
-            packed[:, depth].reshape(tiles, id_rows, depth),
-            jnp.zeros((tiles, (-id_rows) % 8, depth), jnp.float32),
-        ],
-        axis=1,
-    )
+    pad_rows = (-id_rows) % 8
+    table = jnp.concatenate([row_data, jnp.zeros((1, depth), jnp.float32), send_ids.reshape(slots // depth, depth)])
+    chunk_rows = source_row.reshape(tiles, capacity)
+    id_index = row_count + 1 + jnp.arange(tiles * id_rows, dtype=jnp.int32).reshape(tiles, id_rows)
+    pad_index = jnp.full((tiles, pad_rows), row_count, jnp.int32)
+    index = jnp.concatenate([chunk_rows, id_index, pad_index], axis=1).reshape(-1)
+    sendbuf = jnp.take(table, index, axis=0).reshape(tiles, capacity + id_rows + pad_rows, depth)
     arrived_all = lax.all_to_all(sendbuf, "plan", split_axis=0, concat_axis=0, tiled=True)
     arrived = arrived_all[:, :capacity, :]
     arrived_ids = arrived_all[:, capacity:capacity + id_rows, :]

time: 245 us -> 237 us (0.967)
  local copies, waits for them, and re-layouts: 29.1 us -> 24.7 us
  other arithmetic: 13 us -> 9 us
    gather x1, local copies, waits for them, and re-layouts: 16.1 us -> 7.01 us  [per_device(): jnp.take(table, index, axis=0)]
    scatter x1 -> x2, local copies, waits for them, and re-layouts: 4.33 us -> 8.83 us  [the longest x1 4.51 us: per_device(): jnp.full((slots,), float(PATCH_DEV), jnp.float32).at[position]]
    select_n x3, other arithmetic: 5.57 us -> 2.57 us  [the longest x2 1.85 us: per_device(): jnp.take(table, index, axis=0)]
    unnamed x20 -> x16, local copies, waits for them, and re-layouts: 6.24 us -> 6.96 us
where the time goes in v8:
time: 237 us; the launch traced here: 236 us
  Pallas kernels  151 us (64%)
  waiting for transfers between devices  28.4 us (12%)
  local copies, waits for them, and re-layouts  24.7 us (10%)
  starting transfers between devices  17.5 us (7%)
  other arithmetic  9 us (4%)
  matrix products  5.32 us (2%)
    pallas_call x2, Pallas kernels, smooth_each(): pl.pallas_call(functools.partial(filter_kernel, n_plan, n_draw), out_shap...  135 us
    all_to_all x1, waiting for transfers between devices, per_device(): lax.all_to_all(sendbuf, 'plan', split_axis=0, concat_axis=0, tiled=True)  28.4 us
    all_to_all x1, starting transfers between devices, per_device(): lax.all_to_all(sendbuf, 'plan', split_axis=0, concat_axis=0, tiled=True)  17.5 us
    pallas_call x2, Pallas kernels, entering(): pl.pallas_call(functools.partial(scan_kernel, n_draw, reverse), out_shape...  15.7 us
    gather x1, local copies, waits for them, and re-layouts, per_device(): jnp.take(table, index, axis=0)  7.01 us
    unnamed x16, local copies, waits for them, and re-layouts  6.96 us
    dot_general x1, matrix products, per_device(): jnp.dot(picks, arrived.reshape(tiles * capacity, depth), precision=lax.Pr...  4.79 us
  transfers between devices with their start and end apart: 1, of which 1 were waited for; matrix products, arithmetic and copies ran while one was open for 1% of the time, Pallas kernels for 0%

profile of v8, /device:TPU:1, one launch (start us, length us, event | category | flops | bytes accessed | tf_op | source)
XLA Modules:
  0.0 236.4 jit_solution(2086943678359267287)
XLA Ops:
  0.6 0.0 copy-start.2
  0.7 1.4 copy.19.radii_ref
  2.1 0.7 subtract_convert_fusion
  2.8 0.5 fusion.5
  3.3 0.7 compare_select_fusion.2
  4.0 0.1 pad.2.clone
  4.1 4.3 %scatter_custom_fusion = s32[4096]{0:T(1024)S(1)} fusion(s32[1024]{0:T(1024)S(1)} %bitcast.46, s32[1024]{0:T(1024)S(1)} %iota.21, s32[]{:T(128)} %constant.70.clone.1), kind=kCustom, calls=%fused_computation.47 | custom fusion | bytes 16388 | tf_op jit(solution)/shard_map/scatter | solution.py:276
  8.5 0.1 reshape.198
  8.6 0.1 fusion.20
  8.7 2.0 copy.17
  10.7 0.0 copy-done.2
  10.7 0.0 copy-start.3
  10.7 1.0 copy.18
  11.7 68.3 %shard_map.76 = f32[8,128,128]{2,1,0:T(8,128)} custom-call(f32[8,128,128]{2,1,0:T(8,128)} %bitcast.38, s32[8,128,128]{2,1,0:T(8,128)} %bitcast.35, f32[8,3]{1,0:T(8,128)} %copy.19.radii_ref), custom_call_target="tpu_custom_call" | custom-call | tf_op jit(solution)/shard_map/pallas_call | solution.py:214
  80.0 0.0 copy-start
  80.0 1.3 fusion.14
  81.3 0.3 fusion.11
  81.6 0.6 slice_bitcast_fusion.1.part_ref
  82.2 6.8 %shard_map.77 = f32[8,128]{1,0:T(8,128)} custom-call(f32[8,128]{1,0:T(8,128)} %slice_bitcast_fusion.1.part_ref), custom_call_target="tpu_custom_call" | custom-call | tf_op jit(solution)/shard_map/pallas_call | solution.py:67
  89.0 0.0 copy-done.3
  89.0 0.2 copy.21
  89.3 2.1 fusion.6
  91.3 0.6 slice_bitcast_fusion.part_ref
  91.9 8.9 %shard_map.78 = f32[8,128]{1,0:T(8,128)} custom-call(f32[8,128]{1,0:T(8,128)} %slice_bitcast_fusion.part_ref), custom_call_target="tpu_custom_call" | custom-call | tf_op jit(solution)/shard_map/pallas_call | solution.py:67
  100.8 0.0 copy-done
  100.8 1.8 fusion.10.src_ref
  102.6 66.6 %shard_map.79 = f32[8,128,128]{2,1,0:T(8,128)} custom-call(f32[8,128,128]{2,1,0:T(8,128)} %fusion.10.src_ref, s32[8,128,128]{2,1,0:T(8,128)} %bitcast.36, f32[8,3]{1,0:T(8,128)} %copy.19.radii_ref), custom_call_target="tpu_custom_call" | custom-call | tf_op jit(solution)/shard_map/pallas_call | solution.py:214
  169.1 1.2 copy.26
  170.4 0.0 copy-start.1
  170.4 4.5 %scatter_custom_fusion.1 = f32[4096]{0:T(1024)S(1)} fusion(s32[1024]{0:T(1024)S(1)} %bitcast.47, f32[1024]{0:T(1024)S(1)} %get-tuple-element.11, f32[]{:T(128)} %constant.81.clone.1), kind=kCustom, calls=%fused_computation.45 | custom fusion | bytes 16388 | tf_op jit(solution)/shard_map/scatter | solution.py:277
  174.9 0.0 copy-done.1
  174.9 0.3 concatenate.7
  175.2 7.0 %gather_fusion = f32[4352,128]{1,0:T(8,128)S(1)} fusion(f32[1057,128]{1,0:T(8,128)S(1)} %concatenate.7, s32[5120]{0:T(1024)S(1)} %pad_clamp_fusion), kind=kCustom, calls=%fused_computation | custom fusion | bytes 4473856 | tf_op jit(solution)/shard_map/jit(_take)/gather | solution.py:285
  182.3 1.8 broadcast_select_fusion
  184.1 0.0 copy-start.4
  184.1 17.5 %all-to-all-start = ((f32[32,136,128]{2,1,0:T(8,128)}), f32[32,136,128]{2,1,0:T(8,128)S(1)}, u32[]{:S(2)}, u32[]{:S(2)}) async-start(f32[32,136,128]{2,1,0:T(8,128)} %broadcast_select_fusion), calls=%async_computation | async-start | bytes 4456448 | tf_op jit(solution)/shard_map/all_to_all | solution.py:286
  201.6 0.0 copy-done.4
  201.6 0.3 power_bitcast_fusion
  201.9 1.0 copy.25
  202.9 28.4 %all-to-all-done = f32[32,136,128]{2,1,0:T(8,128)S(1)} async-done(((f32[32,136,128]{2,1,0:T(8,128)}), f32[32,136,128]{2,1,0:T(8,128)S(1)}, u32[]{:S(2)}, u32[]{:S(2)}) %all-to-all-start) | async-done | bytes 2228256 | tf_op jit(solution)/shard_map/all_to_all | solution.py:286
  231.3 0.2 slice.21
  231.6 4.8 %fusion.3 = f32[512,128]{1,0:T(8,128)} fusion(f32[4096,128]{1,0:T(8,128)S(1)} %bitcast.39, s32[4096]{0:T(1024)S(1)} %bitcast.45), kind=kOutput, calls=%fused_computation.8 | convolution fusion | flops 3223388160 | bytes 2375680 | tf_op jit(solution)/shard_map/dot_general | solution.py:292
  (8 shorter events, 0.1 us)
Async XLA Ops:
  0.6 10.1 %copy-start.2 = (s32[8,128,128]{2,1,0:T(8,128)S(1)}, s32[8,128,128]{2,1,0:T(8,128)}, u32[]{:S(2)}) copy-start(s32[8,128,128]{2,1,0:T(8,128)} %param.6) | copy-start | bytes 1572868
  10.7 78.3 %copy-start.3 = (f32[8,128,128]{2,1,0:T(8,128)S(1)}, f32[8,128,128]{2,1,0:T(8,128)}, u32[]{:S(2)}) copy-start(f32[8,128,128]{2,1,0:T(8,128)} %param.8) | copy-start | bytes 1572868
  80.0 20.8 %copy-start = (f32[8,128,128]{2,1,0:T(8,128)S(1)}, f32[8,128,128]{2,1,0:T(8,128)}, u32[]{:S(2)}) copy-start(f32[8,128,128]{2,1,0:T(8,128)} %shard_map.76) | copy-start | bytes 1572868
  170.4 4.5 %copy-start.1 = (f32[8,128,128]{2,1,0:T(8,128)}, f32[8,128,128]{2,1,0:T(8,128)S(1)}, u32[]{:S(2)}) copy-start(f32[8,128,128]{2,1,0:T(8,128)S(1)} %copy.26) | copy-start | bytes 1572868
  184.1 17.5 %copy-start.4 = (f32[8,128]{1,0:T(8,128)S(1)}, f32[8,128]{1,0:T(8,128)}, u32[]{:S(2)}) copy-start(f32[8,128]{1,0:T(8,128)} %shard_map.77) | copy-start | bytes 12292
  184.1 47.3 %all-to-all-start = ((f32[32,136,128]{2,1,0:T(8,128)}), f32[32,136,128]{2,1,0:T(8,128)S(1)}, u32[]{:S(2)}, u32[]{:S(2)}) async-start(f32[32,136,128]{2,1,0:T(8,128)} %broadcast_select_fusion), calls=%async_computation | async-start | bytes 4456448 | tf_op jit(solution)/shard_map/all_to_all | solution.py:286

commit v9 on v8

--- a/solution.py
+++ b/solution.py
@@ -273,8 +273,10 @@
     ranking = jnp.sum(counted * onehot.astype(jnp.float32), axis=1).astype(jnp.int32) - 1
     position = owners * capacity + ranking
     slots = tiles * capacity
-    source_row = jnp.full((slots,), row_count, jnp.int32).at[position].set(rows)
-    send_ids = jnp.full((slots,), float(PATCH_DEV), jnp.float32).at[position].set(slot_patch.astype(jnp.float32))
+    key = 2 * PATCH_DEV
+    filled = jnp.full((slots,), row_count * key + PATCH_DEV, jnp.int32).at[position].set(rows * key + slot_patch)
+    source_row = filled // key
+    send_ids = (filled % key).astype(jnp.float32)
     id_rows = capacity // depth
     pad_rows = (-id_rows) % 8
     table = jnp.concatenate([row_data, jnp.zeros((1, depth), jnp.float32), send_ids.reshape(slots // depth, depth)])

time: 237 us -> 233 us (0.983)
  local copies, waits for them, and re-layouts: 24.7 us -> 21 us
    scatter x2 -> x1, local copies, waits for them, and re-layouts: 8.83 us -> 4.33 us  [per_device(): jnp.full((slots,), row_count * key + PATCH_DEV, jnp.int32).at[position]]
where the time goes in v9:
time: 233 us
  Pallas kernels  151 us (65%)
  waiting for transfers between devices  28.4 us (12%)
  local copies, waits for them, and re-layouts  21 us (9%)
  starting transfers between devices  17.5 us (8%)
  other arithmetic  9.02 us (4%)
  matrix products  5.32 us (2%)
    pallas_call x2, Pallas kernels, smooth_each(): pl.pallas_call(functools.partial(filter_kernel, n_plan, n_draw), out_shap...  135 us
    all_to_all x1, waiting for transfers between devices, per_device(): lax.all_to_all(sendbuf, 'plan', split_axis=0, concat_axis=0, tiled=True)  28.4 us
    all_to_all x1, starting transfers between devices, per_device(): lax.all_to_all(sendbuf, 'plan', split_axis=0, concat_axis=0, tiled=True)  17.5 us
    pallas_call x2, Pallas kernels, entering(): pl.pallas_call(functools.partial(scan_kernel, n_draw, reverse), out_shape...  15.7 us
    unnamed x16, local copies, waits for them, and re-layouts  7.73 us
    gather x1, local copies, waits for them, and re-layouts, per_device(): jnp.take(table, index, axis=0)  7 us
    dot_general x1, matrix products, per_device(): jnp.dot(picks, arrived.reshape(tiles * capacity, depth), precision=lax.Pr...  4.79 us
  transfers between devices with their start and end apart: 1, of which 1 were waited for; matrix products, arithmetic and copies ran while one was open for 1% of the time, Pallas kernels for 0%

profile of v9, /device:TPU:1, one launch (start us, length us, event | category | flops | bytes accessed | tf_op | source)
XLA Modules:
  0.0 232.6 jit_solution(6933777517897515246)
XLA Ops:
  0.6 0.0 copy-start.2
  0.7 1.4 copy.19.radii_ref
  2.1 0.7 subtract_add_fusion
  2.8 0.5 fusion.5
  3.3 0.7 compare_select_fusion.2
  4.0 4.3 %scatter_custom_fusion = s32[4096]{0:T(1024)S(1)} fusion(s32[1024]{0:T(1024)S(1)} %bitcast.45, s32[1024]{0:T(1024)S(1)} %get-tuple-element.13, s32[]{:T(128)} %constant.92.clone.1), kind=kCustom, calls=%fused_computation.55 | custom fusion | bytes 16388 | tf_op jit(solution)/shard_map/scatter | solution.py:277
  8.4 0.1 pad.2.clone
  8.5 0.1 reshape.198
  8.6 0.1 fusion.20
  8.7 2.0 copy.17
  10.7 0.0 copy-done.2
  10.7 0.0 copy-start.3
  10.7 1.0 copy.18
  11.7 68.3 %shard_map.76 = f32[8,128,128]{2,1,0:T(8,128)} custom-call(f32[8,128,128]{2,1,0:T(8,128)} %bitcast.39, s32[8,128,128]{2,1,0:T(8,128)} %bitcast.36, f32[8,3]{1,0:T(8,128)} %copy.19.radii_ref), custom_call_target="tpu_custom_call" | custom-call | tf_op jit(solution)/shard_map/pallas_call | solution.py:214
  80.0 0.0 copy-start
  80.0 1.3 fusion.14
  81.3 0.3 fusion.11
  81.6 0.6 slice_bitcast_fusion.1.part_ref
  82.2 6.8 %shard_map.77 = f32[8,128]{1,0:T(8,128)} custom-call(f32[8,128]{1,0:T(8,128)} %slice_bitcast_fusion.1.part_ref), custom_call_target="tpu_custom_call" | custom-call | tf_op jit(solution)/shard_map/pallas_call | solution.py:67
  89.0 0.0 copy-done.3
  89.0 0.2 copy.21
  89.3 2.1 fusion.6
  91.3 0.6 slice_bitcast_fusion.part_ref
  91.9 8.9 %shard_map.78 = f32[8,128]{1,0:T(8,128)} custom-call(f32[8,128]{1,0:T(8,128)} %slice_bitcast_fusion.part_ref), custom_call_target="tpu_custom_call" | custom-call | tf_op jit(solution)/shard_map/pallas_call | solution.py:67
  100.8 0.0 copy-done
  100.8 1.8 fusion.10.src_ref
  102.6 66.6 %shard_map.79 = f32[8,128,128]{2,1,0:T(8,128)} custom-call(f32[8,128,128]{2,1,0:T(8,128)} %fusion.10.src_ref, s32[8,128,128]{2,1,0:T(8,128)} %bitcast.37, f32[8,3]{1,0:T(8,128)} %copy.19.radii_ref), custom_call_target="tpu_custom_call" | custom-call | tf_op jit(solution)/shard_map/pallas_call | solution.py:214
  169.2 1.2 copy.26
  170.4 0.0 copy-start.1
  170.4 0.8 copy-done.1
  171.2 0.3 concatenate.7
  171.5 7.0 %gather_fusion = f32[4352,128]{1,0:T(8,128)S(1)} fusion(f32[1057,128]{1,0:T(8,128)S(1)} %concatenate.7, s32[5120]{0:T(1024)S(1)} %pad_clamp_fusion), kind=kCustom, calls=%fused_computation | custom fusion | bytes 4473856 | tf_op jit(solution)/shard_map/jit(_take)/gather | solution.py:287
  178.5 1.8 broadcast_select_fusion
  180.3 0.0 copy-start.4
  180.3 17.5 %all-to-all-start = ((f32[32,136,128]{2,1,0:T(8,128)}), f32[32,136,128]{2,1,0:T(8,128)S(1)}, u32[]{:S(2)}, u32[]{:S(2)}) async-start(f32[32,136,128]{2,1,0:T(8,128)} %broadcast_select_fusion), calls=%async_computation | async-start | bytes 4456448 | tf_op jit(solution)/shard_map/all_to_all | solution.py:288
  197.9 0.0 copy-done.4
  197.9 0.3 power_bitcast_fusion
  198.1 1.0 copy.25
  199.2 28.4 %all-to-all-done = f32[32,136,128]{2,1,0:T(8,128)S(1)} async-done(((f32[32,136,128]{2,1,0:T(8,128)}), f32[32,136,128]{2,1,0:T(8,128)S(1)}, u32[]{:S(2)}, u32[]{:S(2)}) %all-to-all-start) | async-done | bytes 2228256 | tf_op jit(solution)/shard_map/all_to_all | solution.py:288
  227.6 0.2 slice.21
  227.8 4.8 %fusion.3 = f32[512,128]{1,0:T(8,128)} fusion(f32[4096,128]{1,0:T(8,128)S(1)} %bitcast.40, s32[4096]{0:T(1024)S(1)} %bitcast.44), kind=kOutput, calls=%fused_computation.7 | convolution fusion | flops 3223388160 | bytes 2375680 | tf_op jit(solution)/shard_map/dot_general | solution.py:294
  (8 shorter events, 0.1 us)
Async XLA Ops:
  0.6 10.1 %copy-start.2 = (s32[8,128,128]{2,1,0:T(8,128)S(1)}, s32[8,128,128]{2,1,0:T(8,128)}, u32[]{:S(2)}) copy-start(s32[8,128,128]{2,1,0:T(8,128)} %param.6) | copy-start | bytes 1572868
  10.7 78.3 %copy-start.3 = (f32[8,128,128]{2,1,0:T(8,128)S(1)}, f32[8,128,128]{2,1,0:T(8,128)}, u32[]{:S(2)}) copy-start(f32[8,128,128]{2,1,0:T(8,128)} %param.8) | copy-start | bytes 1572868
  80.0 20.8 %copy-start = (f32[8,128,128]{2,1,0:T(8,128)S(1)}, f32[8,128,128]{2,1,0:T(8,128)}, u32[]{:S(2)}) copy-start(f32[8,128,128]{2,1,0:T(8,128)} %shard_map.76) | copy-start | bytes 1572868
  170.4 0.8 copy-start.1
  180.3 17.5 %copy-start.4 = (f32[8,128]{1,0:T(8,128)S(1)}, f32[8,128]{1,0:T(8,128)}, u32[]{:S(2)}) copy-start(f32[8,128]{1,0:T(8,128)} %shard_map.77) | copy-start | bytes 12292
  180.3 47.2 %all-to-all-start = ((f32[32,136,128]{2,1,0:T(8,128)}), f32[32,136,128]{2,1,0:T(8,128)S(1)}, u32[]{:S(2)}, u32[]{:S(2)}) async-start(f32[32,136,128]{2,1,0:T(8,128)} %broadcast_select_fusion), calls=%async_computation | async-start | bytes 4456448 | tf_op jit(solution)/shard_map/all_to_all | solution.py:288

commit v10 on v9

--- a/solution.py
+++ b/solution.py
@@ -291,7 +291,7 @@
     picks = (
         jnp.arange(PATCH_DEV, dtype=jnp.int32)[:, None] == arrived_ids.reshape(1, tiles * capacity).astype(jnp.int32)
     ).astype(jnp.float32)
-    summed = jnp.dot(picks, arrived.reshape(tiles * capacity, depth), precision=lax.Precision.HIGHEST,
+    summed = jnp.dot(picks, arrived.reshape(tiles * capacity, depth), precision=lax.Precision.HIGH,
                      preferred_element_type=jnp.float32)
     patch_sens = 0.25 * summed
     return (cast_density, filtered_sens, patch_sens)

time: 233 us -> 231 us (level)
  no operation moved by 1% of the time
where the time goes in v10:
time: 231 us
  Pallas kernels  151 us (65%)
  waiting for transfers between devices  28.4 us (12%)
  local copies, waits for them, and re-layouts  21 us (9%)
  starting transfers between devices  17.5 us (8%)
  other arithmetic  9.02 us (4%)
  matrix products  3.58 us (2%)
    pallas_call x2, Pallas kernels, smooth_each(): pl.pallas_call(functools.partial(filter_kernel, n_plan, n_draw), out_shap...  135 us
    all_to_all x1, waiting for transfers between devices, per_device(): lax.all_to_all(sendbuf, 'plan', split_axis=0, concat_axis=0, tiled=True)  28.4 us
    all_to_all x1, starting transfers between devices, per_device(): lax.all_to_all(sendbuf, 'plan', split_axis=0, concat_axis=0, tiled=True)  17.5 us
    pallas_call x2, Pallas kernels, entering(): pl.pallas_call(functools.partial(scan_kernel, n_draw, reverse), out_shape...  15.7 us
    unnamed x16, local copies, waits for them, and re-layouts  7.73 us
    gather x1, local copies, waits for them, and re-layouts, per_device(): jnp.take(table, index, axis=0)  7 us
  transfers between devices with their start and end apart: 1, of which 1 were waited for; matrix products, arithmetic and copies ran while one was open for 1% of the time, Pallas kernels for 0%

profile of v10, /device:TPU:1, one launch (start us, length us, event | category | flops | bytes accessed | tf_op | source)
XLA Modules:
  0.0 230.9 jit_solution(18384369448250290)
XLA Ops:
  0.6 0.0 copy-start.2
  0.7 1.4 copy.19.radii_ref
  2.1 0.7 subtract_add_fusion
  2.8 0.5 fusion.5
  3.3 0.7 compare_select_fusion.2
  4.0 4.3 %scatter_custom_fusion = s32[4096]{0:T(1024)S(1)} fusion(s32[1024]{0:T(1024)S(1)} %bitcast.45, s32[1024]{0:T(1024)S(1)} %get-tuple-element.13, s32[]{:T(128)} %constant.92.clone.1), kind=kCustom, calls=%fused_computation.55 | custom fusion | bytes 16388 | tf_op jit(solution)/shard_map/scatter | solution.py:277
  8.4 0.1 pad.2.clone
  8.5 0.1 reshape.198
  8.6 0.1 fusion.20
  8.7 2.0 copy.17
  10.7 0.0 copy-done.2
  10.7 0.0 copy-start.3
  10.7 1.0 copy.18
  11.7 68.3 %shard_map.76 = f32[8,128,128]{2,1,0:T(8,128)} custom-call(f32[8,128,128]{2,1,0:T(8,128)} %bitcast.39, s32[8,128,128]{2,1,0:T(8,128)} %bitcast.36, f32[8,3]{1,0:T(8,128)} %copy.19.radii_ref), custom_call_target="tpu_custom_call" | custom-call | tf_op jit(solution)/shard_map/pallas_call | solution.py:214
  80.0 0.0 copy-start
  80.0 1.3 fusion.14
  81.3 0.3 fusion.11
  81.6 0.6 slice_bitcast_fusion.1.part_ref
  82.2 6.8 %shard_map.77 = f32[8,128]{1,0:T(8,128)} custom-call(f32[8,128]{1,0:T(8,128)} %slice_bitcast_fusion.1.part_ref), custom_call_target="tpu_custom_call" | custom-call | tf_op jit(solution)/shard_map/pallas_call | solution.py:67
  89.0 0.0 copy-done.3
  89.0 0.2 copy.21
  89.3 2.1 fusion.6
  91.3 0.6 slice_bitcast_fusion.part_ref
  91.9 8.9 %shard_map.78 = f32[8,128]{1,0:T(8,128)} custom-call(f32[8,128]{1,0:T(8,128)} %slice_bitcast_fusion.part_ref), custom_call_target="tpu_custom_call" | custom-call | tf_op jit(solution)/shard_map/pallas_call | solution.py:67
  100.8 0.0 copy-done
  100.8 1.8 fusion.10.src_ref
  102.6 66.6 %shard_map.79 = f32[8,128,128]{2,1,0:T(8,128)} custom-call(f32[8,128,128]{2,1,0:T(8,128)} %fusion.10.src_ref, s32[8,128,128]{2,1,0:T(8,128)} %bitcast.37, f32[8,3]{1,0:T(8,128)} %copy.19.radii_ref), custom_call_target="tpu_custom_call" | custom-call | tf_op jit(solution)/shard_map/pallas_call | solution.py:214
  169.2 1.2 copy.26
  170.4 0.0 copy-start.1
  170.4 0.8 copy-done.1
  171.2 0.3 concatenate.7
  171.5 7.0 %gather_fusion = f32[4352,128]{1,0:T(8,128)S(1)} fusion(f32[1057,128]{1,0:T(8,128)S(1)} %concatenate.7, s32[5120]{0:T(1024)S(1)} %pad_clamp_fusion), kind=kCustom, calls=%fused_computation | custom fusion | bytes 4473856 | tf_op jit(solution)/shard_map/jit(_take)/gather | solution.py:287
  178.5 1.8 broadcast_select_fusion
  180.3 0.0 copy-start.4
  180.3 17.5 %all-to-all-start = ((f32[32,136,128]{2,1,0:T(8,128)}), f32[32,136,128]{2,1,0:T(8,128)S(1)}, u32[]{:S(2)}, u32[]{:S(2)}) async-start(f32[32,136,128]{2,1,0:T(8,128)} %broadcast_select_fusion), calls=%async_computation | async-start | bytes 4456448 | tf_op jit(solution)/shard_map/all_to_all | solution.py:288
  197.9 0.0 copy-done.4
  197.9 0.3 power_bitcast_fusion
  198.1 1.0 copy.25
  199.2 28.4 %all-to-all-done = f32[32,136,128]{2,1,0:T(8,128)S(1)} async-done(((f32[32,136,128]{2,1,0:T(8,128)}), f32[32,136,128]{2,1,0:T(8,128)S(1)}, u32[]{:S(2)}, u32[]{:S(2)}) %all-to-all-start) | async-done | bytes 2228256 | tf_op jit(solution)/shard_map/all_to_all | solution.py:288
  227.6 0.2 slice.21
  227.8 3.0 %fusion.3 = f32[512,128]{1,0:T(8,128)} fusion(f32[4096,128]{1,0:T(8,128)S(1)} %bitcast.40, s32[4096]{0:T(1024)S(1)} %bitcast.44), kind=kOutput, calls=%fused_computation.7 | convolution fusion | flops 1612775424 | bytes 2375680 | tf_op jit(solution)/shard_map/dot_general | solution.py:294
  (8 shorter events, 0.1 us)
Async XLA Ops:
  0.6 10.1 %copy-start.2 = (s32[8,128,128]{2,1,0:T(8,128)S(1)}, s32[8,128,128]{2,1,0:T(8,128)}, u32[]{:S(2)}) copy-start(s32[8,128,128]{2,1,0:T(8,128)} %param.6) | copy-start | bytes 1572868
  10.7 78.3 %copy-start.3 = (f32[8,128,128]{2,1,0:T(8,128)S(1)}, f32[8,128,128]{2,1,0:T(8,128)}, u32[]{:S(2)}) copy-start(f32[8,128,128]{2,1,0:T(8,128)} %param.8) | copy-start | bytes 1572868
  80.0 20.8 %copy-start = (f32[8,128,128]{2,1,0:T(8,128)S(1)}, f32[8,128,128]{2,1,0:T(8,128)}, u32[]{:S(2)}) copy-start(f32[8,128,128]{2,1,0:T(8,128)} %shard_map.76) | copy-start | bytes 1572868
  170.4 0.8 copy-start.1
  180.3 17.5 %copy-start.4 = (f32[8,128]{1,0:T(8,128)S(1)}, f32[8,128]{1,0:T(8,128)}, u32[]{:S(2)}) copy-start(f32[8,128]{1,0:T(8,128)} %shard_map.77) | copy-start | bytes 12292
  180.3 47.2 %all-to-all-start = ((f32[32,136,128]{2,1,0:T(8,128)}), f32[32,136,128]{2,1,0:T(8,128)S(1)}, u32[]{:S(2)}, u32[]{:S(2)}) async-start(f32[32,136,128]{2,1,0:T(8,128)} %broadcast_select_fusion), calls=%async_computation | async-start | bytes 4456448 | tf_op jit(solution)/shard_map/all_to_all | solution.py:288

commit v11 on v10

--- a/solution.py
+++ b/solution.py
@@ -78,11 +78,12 @@
     )(part)
 
 
-def filter_kernel(n_plan, n_draw, src_ref, ids_ref, radii_ref, out_ref, field, cx_ref, cy_ref, cz_ref, inv_ref,
-                  send_sem, recv_sem):
+def filter_kernel(n_plan, n_draw, turn_src, src_in, ids_ref, radii_ref, out_ref, field, cx_ref, cy_ref, cz_ref,
+                  inv_ref, src_ref, send_sem, recv_sem):
     planes, depth, width = src_ref.shape
     for i in range(planes):
-        cls = ids_ref[i]
+        src_ref[i] = src_in[i].T if turn_src else src_in[i]
+        cls = ids_ref[i].T
         cx = jnp.zeros((depth, width), jnp.float32)
         cy = jnp.zeros((depth, width), jnp.float32)
         cz = jnp.zeros((depth, width), jnp.float32)
@@ -207,12 +208,12 @@
         update(1, i, 0, depth, True)
 
 
-def smooth_each(source, class_ids, class_radii, n_plan, n_draw, kid):
+def smooth_each(source, class_ids, class_radii, n_plan, n_draw, kid, turn_src):
     planes, depth, width = source.shape
     vmem = pl.BlockSpec(memory_space=pltpu.VMEM)
     smem = pl.BlockSpec(memory_space=pltpu.SMEM)
     return pl.pallas_call(
-        functools.partial(filter_kernel, n_plan, n_draw),
+        functools.partial(filter_kernel, n_plan, n_draw, turn_src),
         out_shape=jax.ShapeDtypeStruct(source.shape, jnp.float32),
         in_specs=[vmem, vmem, smem],
         out_specs=vmem,
@@ -222,6 +223,7 @@
             pltpu.VMEM(source.shape, jnp.float32),
             pltpu.VMEM(source.shape, jnp.float32),
             pltpu.VMEM(source.shape, jnp.float32),
+            pltpu.VMEM(source.shape, jnp.float32),
             pltpu.SemaphoreType.DMA((2, 4)),
             pltpu.SemaphoreType.DMA((2, 4)),
         ],
@@ -230,10 +232,8 @@
 
 
 def per_device(n_plan, n_draw, design, class_ids, class_radii, sensitivity, row_patch):
-    design_t = jnp.swapaxes(design, 1, 2)
-    ids_t = jnp.swapaxes(class_ids, 1, 2)
     sens_t = jnp.swapaxes(sensitivity, 1, 2)
-    filtered = smooth_each(design_t, ids_t, class_radii, n_plan, n_draw, 0)
+    filtered = smooth_each(design, class_ids, class_radii, n_plan, n_draw, 0, True)
     denom = jnp.tanh(jnp.float32(BETA * ETA)) + jnp.tanh(jnp.float32(BETA * (1.0 - ETA)))
     steep = jnp.tanh(BETA * (filtered - ETA))
     projected = RMIN + (1.0 - RMIN) * (jnp.tanh(jnp.float32(BETA * ETA)) + steep) / denom
@@ -255,7 +255,7 @@
         * (1.0 - steep * steep)
         / denom
     )
-    filtered_sens_t = smooth_each(chained, ids_t, class_radii, n_plan, n_draw, 1)
+    filtered_sens_t = smooth_each(chained, class_ids, class_radii, n_plan, n_draw, 1, False)
     filtered_sens = jnp.swapaxes(filtered_sens_t, 1, 2)
     cast_density = jnp.swapaxes(cast_density, 1, 2)
     depth = filtered_sens.shape[2]

time: 231 us -> 228 us (0.987)
  local copies, waits for them, and re-layouts: 21 us -> 17.9 us
    unnamed x16 -> x12, local copies, waits for them, and re-layouts: 7.73 us -> 4.64 us
where the time goes in v11:
time: 228 us
  Pallas kernels  150 us (66%)
  waiting for transfers between devices  28.4 us (12%)
  local copies, waits for them, and re-layouts  17.9 us (8%)
  starting transfers between devices  17.5 us (8%)
  other arithmetic  9.07 us (4%)
  matrix products  3.57 us (2%)
    pallas_call x2, Pallas kernels, smooth_each(): pl.pallas_call(functools.partial(filter_kernel, n_plan, n_draw, turn_src)...  135 us
    all_to_all x1, waiting for transfers between devices, per_device(): lax.all_to_all(sendbuf, 'plan', split_axis=0, concat_axis=0, tiled=True)  28.4 us
    all_to_all x1, starting transfers between devices, per_device(): lax.all_to_all(sendbuf, 'plan', split_axis=0, concat_axis=0, tiled=True)  17.5 us
    pallas_call x2, Pallas kernels, entering(): pl.pallas_call(functools.partial(scan_kernel, n_draw, reverse), out_shape...  15.7 us
    gather x1, local copies, waits for them, and re-layouts, per_device(): jnp.take(table, index, axis=0)  7.01 us
    unnamed x12, local copies, waits for them, and re-layouts  4.64 us
  transfers between devices with their start and end apart: 1, of which 1 were waited for; matrix products, arithmetic and copies ran while one was open for 1% of the time, Pallas kernels for 0%

profile of v11, /device:TPU:1, one launch (start us, length us, event | category | flops | bytes accessed | tf_op | source)
XLA Modules:
  0.0 227.6 jit_solution(13080582006747309866)
XLA Ops:
  0.6 1.4 copy.15.radii_ref
  2.0 0.7 subtract_add_fusion
  2.7 0.5 fusion.5
  3.2 0.0 copy-start.2
  3.3 0.8 compare_select_fusion.2
  4.0 4.3 %scatter_custom_fusion = s32[4096]{0:T(1024)S(1)} fusion(s32[1024]{0:T(1024)S(1)} %bitcast.40, s32[1024]{0:T(1024)S(1)} %get-tuple-element.13, s32[]{:T(128)} %constant.92.clone.1), kind=kCustom, calls=%fused_computation.55 | custom fusion | bytes 16388 | tf_op jit(solution)/shard_map/scatter | solution.py:277
  8.4 0.1 pad.2.clone
  8.5 0.1 reshape.198
  8.6 0.1 fusion.20
  8.7 68.2 %shard_map.76 = f32[8,128,128]{2,1,0:T(8,128)} custom-call(f32[8,128,128]{2,1,0:T(8,128)} %src_in.1, s32[8,128,128]{2,1,0:T(8,128)} %ids_ref.3, f32[8,3]{1,0:T(8,128)} %copy.15.radii_ref), custom_call_target="tpu_custom_call" | custom-call | tf_op jit(solution)/shard_map/pallas_call | solution.py:215
  76.9 0.0 copy-start
  76.9 1.3 fusion.14
  78.2 0.3 fusion.11
  78.5 0.6 slice_bitcast_fusion.1.part_ref
  79.1 6.8 %shard_map.77 = f32[8,128]{1,0:T(8,128)} custom-call(f32[8,128]{1,0:T(8,128)} %slice_bitcast_fusion.1.part_ref), custom_call_target="tpu_custom_call" | custom-call | tf_op jit(solution)/shard_map/pallas_call | solution.py:67
  85.9 0.0 copy-done.2
  85.9 0.2 copy.17
  86.2 2.1 fusion.6
  88.2 0.6 slice_bitcast_fusion.part_ref
  88.8 8.9 %shard_map.78 = f32[8,128]{1,0:T(8,128)} custom-call(f32[8,128]{1,0:T(8,128)} %slice_bitcast_fusion.part_ref), custom_call_target="tpu_custom_call" | custom-call | tf_op jit(solution)/shard_map/pallas_call | solution.py:67
  97.7 0.0 copy-done
  97.7 1.8 fusion.10.src_in
  99.5 66.4 %shard_map.79 = f32[8,128,128]{2,1,0:T(8,128)} custom-call(f32[8,128,128]{2,1,0:T(8,128)} %fusion.10.src_in, s32[8,128,128]{2,1,0:T(8,128)} %ids_ref.3, f32[8,3]{1,0:T(8,128)} %copy.15.radii_ref), custom_call_target="tpu_custom_call" | custom-call | tf_op jit(solution)/shard_map/pallas_call | solution.py:215
  165.9 1.2 copy.22
  167.1 0.0 copy-start.1
  167.2 0.8 copy-done.1
  167.9 0.3 concatenate.7
  168.2 7.0 %gather_fusion = f32[4352,128]{1,0:T(8,128)S(1)} fusion(f32[1057,128]{1,0:T(8,128)S(1)} %concatenate.7, s32[5120]{0:T(1024)S(1)} %pad_clamp_fusion), kind=kCustom, calls=%fused_computation | custom fusion | bytes 4473856 | tf_op jit(solution)/shard_map/jit(_take)/gather | solution.py:287
  175.2 1.8 broadcast_select_fusion
  177.0 0.0 copy-start.3
  177.0 17.5 %all-to-all-start = ((f32[32,136,128]{2,1,0:T(8,128)}), f32[32,136,128]{2,1,0:T(8,128)S(1)}, u32[]{:S(2)}, u32[]{:S(2)}) async-start(f32[32,136,128]{2,1,0:T(8,128)} %broadcast_select_fusion), calls=%async_computation | async-start | bytes 4456448 | tf_op jit(solution)/shard_map/all_to_all | solution.py:288
  194.6 0.0 copy-done.3
  194.6 0.3 power_bitcast_fusion
  194.9 1.0 copy.21
  195.9 28.4 %all-to-all-done = f32[32,136,128]{2,1,0:T(8,128)S(1)} async-done(((f32[32,136,128]{2,1,0:T(8,128)}), f32[32,136,128]{2,1,0:T(8,128)S(1)}, u32[]{:S(2)}, u32[]{:S(2)}) %all-to-all-start) | async-done | bytes 2228256 | tf_op jit(solution)/shard_map/all_to_all | solution.py:288
  224.3 0.2 slice.21
  224.6 3.0 %fusion.3 = f32[512,128]{1,0:T(8,128)} fusion(f32[4096,128]{1,0:T(8,128)S(1)} %bitcast.35, s32[4096]{0:T(1024)S(1)} %bitcast.39), kind=kOutput, calls=%fused_computation.7 | convolution fusion | flops 1612775424 | bytes 2375680 | tf_op jit(solution)/shard_map/dot_general | solution.py:294
  (8 shorter events, 0.1 us)
Async XLA Ops:
  3.2 82.7 %copy-start.2 = (f32[8,128,128]{2,1,0:T(8,128)S(1)}, f32[8,128,128]{2,1,0:T(8,128)}, u32[]{:S(2)}) copy-start(f32[8,128,128]{2,1,0:T(8,128)} %param.8) | copy-start | bytes 1572868
  76.9 20.8 %copy-start = (f32[8,128,128]{2,1,0:T(8,128)S(1)}, f32[8,128,128]{2,1,0:T(8,128)}, u32[]{:S(2)}) copy-start(f32[8,128,128]{2,1,0:T(8,128)} %shard_map.76) | copy-start | bytes 1572868
  167.1 0.8 copy-start.1
  177.0 17.6 %copy-start.3 = (f32[8,128]{1,0:T(8,128)S(1)}, f32[8,128]{1,0:T(8,128)}, u32[]{:S(2)}) copy-start(f32[8,128]{1,0:T(8,128)} %shard_map.77) | copy-start | bytes 12292
  177.0 47.2 %all-to-all-start = ((f32[32,136,128]{2,1,0:T(8,128)}), f32[32,136,128]{2,1,0:T(8,128)S(1)}, u32[]{:S(2)}, u32[]{:S(2)}) async-start(f32[32,136,128]{2,1,0:T(8,128)} %broadcast_select_fusion), calls=%async_computation | async-start | bytes 4456448 | tf_op jit(solution)/shard_map/all_to_all | solution.py:288

commit v12 on v11

--- a/solution.py
+++ b/solution.py
@@ -163,8 +163,10 @@
         part = pl.ds(r0, rows)
         new = (src_ref[i, part, :] + cx_ref[i, part, :] * (xm + xp) + cy_ref[i, part, :] * (ym + yp)
                + cz_ref[i, part, :] * (zm + zp)) * inv_ref[i, part, :]
-        if last:
+        if last and turn_src:
             out_ref[i, part, :] = new
+        elif last:
+            out_ref[i] = new.T
         else:
             field[1 - s, i + 1, pl.ds(at, rows), :] = new
 
@@ -256,7 +258,7 @@
         / denom
     )
     filtered_sens_t = smooth_each(chained, class_ids, class_radii, n_plan, n_draw, 1, False)
-    filtered_sens = jnp.swapaxes(filtered_sens_t, 1, 2)
+    filtered_sens = filtered_sens_t
     cast_density = jnp.swapaxes(cast_density, 1, 2)
     depth = filtered_sens.shape[2]
     row_count = filtered_sens.shape[0] * filtered_sens.shape[1]

time: 228 us -> 228 us (level)
  no operation moved by 1% of the time
where the time goes in v12:
time: 228 us
  Pallas kernels  151 us (66%)
  waiting for transfers between devices  28.4 us (12%)
  local copies, waits for them, and re-layouts  17.6 us (8%)
  starting transfers between devices  17.5 us (8%)
  other arithmetic  9.06 us (4%)
  matrix products  3.57 us (2%)
    pallas_call x2, Pallas kernels, smooth_each(): pl.pallas_call(functools.partial(filter_kernel, n_plan, n_draw, turn_src)...  135 us
    all_to_all x1, waiting for transfers between devices, per_device(): lax.all_to_all(sendbuf, 'plan', split_axis=0, concat_axis=0, tiled=True)  28.4 us
    all_to_all x1, starting transfers between devices, per_device(): lax.all_to_all(sendbuf, 'plan', split_axis=0, concat_axis=0, tiled=True)  17.5 us
    pallas_call x2, Pallas kernels, entering(): pl.pallas_call(functools.partial(scan_kernel, n_draw, reverse), out_shape...  15.7 us
    gather x1, local copies, waits for them, and re-layouts, per_device(): jnp.take(table, index, axis=0)  7.01 us
  transfers between devices with their start and end apart: 1, of which 1 were waited for; matrix products, arithmetic and copies ran while one was open for 1% of the time, Pallas kernels for 0%

profile of v12, /device:TPU:1, one launch (start us, length us, event | category | flops | bytes accessed | tf_op | source)
XLA Modules:
  0.0 227.6 jit_solution(7863061209821728745)
XLA Ops:
  0.6 1.4 copy.14.radii_ref
  2.0 0.7 subtract_add_fusion
  2.7 0.5 fusion.5
  3.2 0.0 copy-start.2
  3.3 0.8 compare_select_fusion.2
  4.0 4.3 %scatter_custom_fusion = s32[4096]{0:T(1024)S(1)} fusion(s32[1024]{0:T(1024)S(1)} %bitcast.38, s32[1024]{0:T(1024)S(1)} %get-tuple-element.13, s32[]{:T(128)} %constant.92.clone.1), kind=kCustom, calls=%fused_computation.55 | custom fusion | bytes 16388 | tf_op jit(solution)/shard_map/scatter | solution.py:279
  8.4 0.1 pad.2.clone
  8.5 0.1 reshape.198
  8.6 0.1 fusion.20
  8.7 68.2 %shard_map.76 = f32[8,128,128]{2,1,0:T(8,128)} custom-call(f32[8,128,128]{2,1,0:T(8,128)} %src_in.1, s32[8,128,128]{2,1,0:T(8,128)} %ids_ref.3, f32[8,3]{1,0:T(8,128)} %copy.14.radii_ref), custom_call_target="tpu_custom_call" | custom-call | tf_op jit(solution)/shard_map/pallas_call | solution.py:217
  76.9 0.0 copy-start
  76.9 1.3 fusion.14
  78.2 0.3 fusion.11
  78.5 0.6 slice_bitcast_fusion.1.part_ref
  79.1 6.8 %shard_map.77 = f32[8,128]{1,0:T(8,128)} custom-call(f32[8,128]{1,0:T(8,128)} %slice_bitcast_fusion.1.part_ref), custom_call_target="tpu_custom_call" | custom-call | tf_op jit(solution)/shard_map/pallas_call | solution.py:67
  85.9 0.0 copy-done.2
  85.9 0.2 copy.16
  86.2 2.0 fusion.6
  88.2 0.6 slice_bitcast_fusion.part_ref
  88.8 8.9 %shard_map.78 = f32[8,128]{1,0:T(8,128)} custom-call(f32[8,128]{1,0:T(8,128)} %slice_bitcast_fusion.part_ref), custom_call_target="tpu_custom_call" | custom-call | tf_op jit(solution)/shard_map/pallas_call | solution.py:67
  97.7 0.0 copy-done
  97.7 1.8 fusion.10.src_in
  99.5 66.6 %shard_map.79 = f32[8,128,128]{2,1,0:T(8,128)} custom-call(f32[8,128,128]{2,1,0:T(8,128)} %fusion.10.src_in, s32[8,128,128]{2,1,0:T(8,128)} %ids_ref.3, f32[8,3]{1,0:T(8,128)} %copy.14.radii_ref), custom_call_target="tpu_custom_call" | custom-call | tf_op jit(solution)/shard_map/pallas_call | solution.py:217
  166.1 1.2 concatenate.7
  167.4 7.0 %gather_fusion = f32[4352,128]{1,0:T(8,128)S(1)} fusion(f32[1057,128]{1,0:T(8,128)S(1)} %concatenate.7, s32[5120]{0:T(1024)S(1)} %pad_clamp_fusion), kind=kCustom, calls=%fused_computation | custom fusion | bytes 4473856 | tf_op jit(solution)/shard_map/jit(_take)/gather | solution.py:289
  174.4 1.8 broadcast_select_fusion
  176.2 0.0 copy-start.3
  176.2 17.5 %all-to-all-start = ((f32[32,136,128]{2,1,0:T(8,128)}), f32[32,136,128]{2,1,0:T(8,128)S(1)}, u32[]{:S(2)}, u32[]{:S(2)}) async-start(f32[32,136,128]{2,1,0:T(8,128)} %broadcast_select_fusion), calls=%async_computation | async-start | bytes 4456448 | tf_op jit(solution)/shard_map/all_to_all | solution.py:290
  193.7 0.0 copy-done.3
  193.8 0.3 power_bitcast_fusion
  194.0 1.0 copy.19
  195.1 28.4 %all-to-all-done = f32[32,136,128]{2,1,0:T(8,128)S(1)} async-done(((f32[32,136,128]{2,1,0:T(8,128)}), f32[32,136,128]{2,1,0:T(8,128)S(1)}, u32[]{:S(2)}, u32[]{:S(2)}) %all-to-all-start) | async-done | bytes 2228256 | tf_op jit(solution)/shard_map/all_to_all | solution.py:290
  223.5 0.2 slice.21
  223.7 0.0 copy-start.1
  223.7 3.0 %fusion.3 = f32[512,128]{1,0:T(8,128)} fusion(f32[4096,128]{1,0:T(8,128)S(1)} %bitcast.34, s32[4096]{0:T(1024)S(1)} %bitcast.37), kind=kOutput, calls=%fused_computation.7 | convolution fusion | flops 1612775424 | bytes 2375680 | tf_op jit(solution)/shard_map/dot_general | solution.py:296
  226.8 0.0 copy-done.1
  226.8 0.8 copy.32
  (8 shorter events, 0.1 us)
Async XLA Ops:
  3.2 82.7 %copy-start.2 = (f32[8,128,128]{2,1,0:T(8,128)S(1)}, f32[8,128,128]{2,1,0:T(8,128)}, u32[]{:S(2)}) copy-start(f32[8,128,128]{2,1,0:T(8,128)} %param.8) | copy-start | bytes 1572868
  76.9 20.8 %copy-start = (f32[8,128,128]{2,1,0:T(8,128)S(1)}, f32[8,128,128]{2,1,0:T(8,128)}, u32[]{:S(2)}) copy-start(f32[8,128,128]{2,1,0:T(8,128)} %shard_map.76) | copy-start | bytes 1572868
  176.2 17.6 %copy-start.3 = (f32[8,128]{1,0:T(8,128)S(1)}, f32[8,128]{1,0:T(8,128)}, u32[]{:S(2)}) copy-start(f32[8,128]{1,0:T(8,128)} %shard_map.77) | copy-start | bytes 12292
  176.2 47.2 %all-to-all-start = ((f32[32,136,128]{2,1,0:T(8,128)}), f32[32,136,128]{2,1,0:T(8,128)S(1)}, u32[]{:S(2)}, u32[]{:S(2)}) async-start(f32[32,136,128]{2,1,0:T(8,128)} %broadcast_select_fusion), calls=%async_computation | async-start | bytes 4456448 | tf_op jit(solution)/shard_map/all_to_all | solution.py:290
  223.7 3.0 %copy-start.1 = (f32[8,128,128]{2,1,0:T(8,128)S(1)}, f32[8,128,128]{2,1,0:T(8,128)}, u32[]{:S(2)}) copy-start(f32[8,128,128]{2,1,0:T(8,128)} %shard_map.79) | copy-start | bytes 1572868
